TPU v7x, 32 devices: a whole 2x2x4 slice. The times are simulated.
32 devices in a mesh: dp: 4 (over x, core), seq: 8 (over z, y).
Axes of the slice: x: 2, y: 2, z: 4, core: 2. Of those that a mesh axis runs over, the one named last changes fastest.
Arguments:
- tokens: bfloat16 [2048, 4, 768], P('seq', 'dp'), may hold values from -6 to 6
- memory: bfloat16 [1536, 4, 768], P(None, 'dp'), may hold values from -6 to 6
- piece_starts: int32 [4, 3], P('dp'), may hold values from 0 to 1792, as said below
- memory_lengths: int32 [4], P('dp'), may hold values from 384 to 1536, as said below
- self_gain: bfloat16 [768], P(('dp', 'seq')), may hold values from 0.25 to 1.75
- self_shift: bfloat16 [768], P(('dp', 'seq')), may hold values from -3 to 3
- query_weight: bfloat16 [768, 768], P(('dp', 'seq')), may hold values from -0.21875 to 0.21875
- query_bias: bfloat16 [768], P(('dp', 'seq')), may hold values from -3 to 3
- key_weight: bfloat16 [768, 768], P(('dp', 'seq')), may hold values from -0.21875 to 0.21875
- value_weight: bfloat16 [768, 768], P(('dp', 'seq')), may hold values from -0.21875 to 0.21875
- value_bias: bfloat16 [768], P(('dp', 'seq')), may hold values from -3 to 3
- attn_out_weight: bfloat16 [768, 768], P(('dp', 'seq')), may hold values from -0.875 to 0.875
- attn_out_bias: bfloat16 [768], P(('dp', 'seq')), may hold values from -3 to 3
- cross_gain: bfloat16 [768], P(('dp', 'seq')), may hold values from 0.25 to 1.75
- cross_shift: bfloat16 [768], P(('dp', 'seq')), may hold values from -3 to 3
- cross_query_weight: bfloat16 [768, 768], P(('dp', 'seq')), may hold values from -0.21875 to 0.21875
- cross_query_bias: bfloat16 [768], P(('dp', 'seq')), may hold values from -3 to 3
- cross_key_weight: bfloat16 [768, 768], P(('dp', 'seq')), may hold values from -0.21875 to 0.21875
- cross_value_weight: bfloat16 [768, 768], P(('dp', 'seq')), may hold values from -0.21875 to 0.21875
- cross_value_bias: bfloat16 [768], P(('dp', 'seq')), may hold values from -3 to 3
- cross_out_weight: bfloat16 [768, 768], P(('dp', 'seq')), may hold values from -0.875 to 0.875
- cross_out_bias: bfloat16 [768], P(('dp', 'seq')), may hold values from -3 to 3
- mlp_gain: bfloat16 [768], P(('dp', 'seq')), may hold values from 0.25 to 1.75
- mlp_shift: bfloat16 [768], P(('dp', 'seq')), may hold values from -3 to 3
- fc_in_weight: bfloat16 [768, 3072], P(('dp', 'seq')), may hold values from -0.21875 to 0.21875
- fc_in_bias: bfloat16 [3072], P(('dp', 'seq')), may hold values from -3 to 3
- fc_out_weight: bfloat16 [3072, 768], P(('dp', 'seq')), may hold values from -0.109375 to 0.109375
- fc_out_bias: bfloat16 [768], P(('dp', 'seq')), may hold values from -3 to 3
- out_grad: float32 [2048, 4, 768], P('seq', 'dp'), may hold values from -6 to 6
Outputs:
- output: bfloat16 [2048, 4, 768], P('seq', 'dp')
- token_grad: float32 [2048, 4, 768], P('seq', 'dp')
- memory_grad: float32 [1536, 4, 768], P(None, 'dp')
- grad_self_gain: float32 [768], P(('dp', 'seq'))
- grad_self_shift: float32 [768], P(('dp', 'seq'))
- grad_query_weight: float32 [768, 768], P(('dp', 'seq'))
- grad_query_bias: float32 [768], P(('dp', 'seq'))
- grad_key_weight: float32 [768, 768], P(('dp', 'seq'))
- grad_value_weight: float32 [768, 768], P(('dp', 'seq'))
- grad_value_bias: float32 [768], P(('dp', 'seq'))
- grad_attn_out_weight: float32 [768, 768], P(('dp', 'seq'))
- grad_attn_out_bias: float32 [768], P(('dp', 'seq'))
- grad_cross_gain: float32 [768], P(('dp', 'seq'))
- grad_cross_shift: float32 [768], P(('dp', 'seq'))
- grad_cross_query_weight: float32 [768, 768], P(('dp', 'seq'))
- grad_cross_query_bias: float32 [768], P(('dp', 'seq'))
- grad_cross_key_weight: float32 [768, 768], P(('dp', 'seq'))
- grad_cross_value_weight: float32 [768, 768], P(('dp', 'seq'))
- grad_cross_value_bias: float32 [768], P(('dp', 'seq'))
- grad_cross_out_weight: float32 [768, 768], P(('dp', 'seq'))
- grad_cross_out_bias: float32 [768], P(('dp', 'seq'))
- grad_mlp_gain: float32 [768], P(('dp', 'seq'))
- grad_mlp_shift: float32 [768], P(('dp', 'seq'))
- grad_fc_in_weight: float32 [768, 3072], P(('dp', 'seq'))
- grad_fc_in_bias: float32 [3072], P(('dp', 'seq'))
- grad_fc_out_weight: float32 [3072, 768], P(('dp', 'seq'))
- grad_fc_out_bias: float32 [768], P(('dp', 'seq'))
Inputs may be any that keep to these rules, and one draw needn't show every extreme that they name: `piece_starts`: each sequence has 3 audio-prompt pieces of 256 positions; each starts at a multiple of 128, the pieces of one sequence don't intersect and each lies inside the sequence. `memory_lengths`: frames at or beyond a sequence's length are padding; some sequence uses all 1536 frames.
All inputs are finite; a program needn't handle non-finite values.
Results may differ from a plain program's by a relative error of at most 0.035.
Values may be sent and summed in bfloat16 or wider, within the bound.
No kernel may reach another device: no remote copies, remote signals or barrier semaphores. Data moves between devices by JAX's collectives and lax.ppermute only.
A program may use at most 256 MiB of HBM per device.

v0:
```python
import math

import jax
import jax.numpy as jnp
from jax import lax
from jax.sharding import PartitionSpec as P

D = 768
HEADS = 12
HEAD = 64
PIECE = 256


norm_epsilon = 1e-05
neg_large = -1e30


def rounded(tensor):
    return tensor.astype(jnp.bfloat16)


def project(left_rows, matrix):
    return jnp.dot(left_rows, matrix, preferred_element_type=jnp.float32)


def project_back(left_rows, matrix):
    return lax.dot_general(
        left_rows, matrix, (((1,), (1,)), ((), ())), preferred_element_type=jnp.float32
    )


def weight_grad(inputs, grad_rows):
    return lax.dot_general(
        inputs, grad_rows, (((0,), (0,)), ((), ())), preferred_element_type=jnp.float32
    )


def column_sums(grad_rows):
    return jnp.sum(grad_rows.astype(jnp.float32), axis=0)


def exact_gelu(inputs):
    return jax.nn.gelu(inputs, approximate=False)


def norm_forward(token_rows, norm_gain, norm_shift):
    centre = token_rows - jnp.mean(token_rows, axis=-1, keepdims=True)
    inverse = lax.rsqrt(jnp.mean(centre * centre, axis=-1, keepdims=True) + norm_epsilon)
    scaled = centre * inverse
    return (scaled * norm_gain + norm_shift, scaled, inverse)


def norm_backward(grad_normed, scaled, inverse, norm_gain):
    grad_scaled = grad_normed * norm_gain
    mean_grad = jnp.mean(grad_scaled, axis=-1, keepdims=True)
    mean_cross = jnp.mean(grad_scaled * scaled, axis=-1, keepdims=True)
    grad_input = inverse * (grad_scaled - mean_grad - scaled * mean_cross)
    return (grad_input, jnp.sum(grad_normed * scaled, axis=0), jnp.sum(grad_normed, axis=0))


def piece_labels(positions, starts):
    inside = (positions[None, :, None] >= starts[:, None, :]) & (
        positions[None, :, None] < starts[:, None, :] + PIECE
    )
    numbers = jnp.arange(1, starts.shape[1] + 1, dtype=jnp.int32)
    return jnp.sum(jnp.where(inside, numbers, 0), axis=2)


def visible(query_pos, query_label, key_pos, key_label):
    causal = (key_pos[None, :] <= query_pos[:, None])[:, None, :]
    query_side = jnp.transpose(query_label)[:, :, None]
    same_piece = (query_side == key_label[None, :, :]) & (query_side > 0)
    return (causal | same_piece)[:, :, None, :]


def local(
    tokens,
    memory,
    piece_starts,
    memory_lengths,
    self_gain,
    self_shift,
    query_weight,
    query_bias,
    key_weight,
    value_weight,
    value_bias,
    attn_out_weight,
    attn_out_bias,
    cross_gain,
    cross_shift,
    cross_query_weight,
    cross_query_bias,
    cross_key_weight,
    cross_value_weight,
    cross_value_bias,
    cross_out_weight,
    cross_out_bias,
    mlp_gain,
    mlp_shift,
    fc_in_weight,
    fc_in_bias,
    fc_out_weight,
    fc_out_bias,
    out_grad,
):
    local_len, batch_count, model_width = tokens.shape
    seq_count = lax.axis_size("seq")
    seq_index = lax.axis_index("seq")
    full_length = local_len * seq_count
    token_count = local_len * batch_count
    query_pos = seq_index * local_len + jnp.arange(local_len, dtype=jnp.int32)
    query_label = piece_labels(query_pos, piece_starts)
    input_rows = tokens.reshape(token_count, D).astype(jnp.float32)
    (
        full_self_gain,
        full_self_shift,
        full_query,
        full_query_bias,
        full_key,
        full_value,
        full_value_bias,
        full_self_out,
        full_self_out_bias,
    ) = (
        lax.all_gather(self_gain, ("dp", "seq"), axis=0, tiled=True),
        lax.all_gather(self_shift, ("dp", "seq"), axis=0, tiled=True),
        lax.all_gather(query_weight, ("dp", "seq"), axis=0, tiled=True),
        lax.all_gather(query_bias, ("dp", "seq"), axis=0, tiled=True),
        lax.all_gather(key_weight, ("dp", "seq"), axis=0, tiled=True),
        lax.all_gather(value_weight, ("dp", "seq"), axis=0, tiled=True),
        lax.all_gather(value_bias, ("dp", "seq"), axis=0, tiled=True),
        lax.all_gather(attn_out_weight, ("dp", "seq"), axis=0, tiled=True),
        lax.all_gather(attn_out_bias, ("dp", "seq"), axis=0, tiled=True),
    )
    normed_self, scaled_self, inverse_self = norm_forward(
        input_rows, full_self_gain.astype(jnp.float32), full_self_shift.astype(jnp.float32)
    )
    normed_self_low = rounded(normed_self)
    query_rows = rounded(project(normed_self_low, full_query) + full_query_bias.astype(jnp.float32))
    key_rows = rounded(project(normed_self_low, full_key)).reshape(local_len, batch_count, D)
    value_rows = rounded(
        project(normed_self_low, full_value) + full_value_bias.astype(jnp.float32)
    ).reshape(local_len, batch_count, D)
    query_heads = query_rows.reshape(local_len, batch_count, HEADS, HEAD)

    def key_block_scores(key_block, key_pos):
        key_heads = key_block.reshape(key_block.shape[0], batch_count, HEADS, HEAD)
        raw_scores = jnp.einsum(
            "qbhd,kbhd->qbhk", query_heads, key_heads, preferred_element_type=jnp.float32
        )
        allowed = visible(query_pos, query_label, key_pos, piece_labels(key_pos, piece_starts))
        return (raw_scores * 0.125, allowed)

    start_state = (
        jnp.full((local_len, batch_count, HEADS), neg_large, jnp.float32),
        jnp.zeros((local_len, batch_count, HEADS), jnp.float32),
        jnp.zeros((local_len, batch_count, HEADS, HEAD), jnp.float32),
    )
    running = start_state
    key_piece = lax.all_gather(key_rows, "seq", axis=0, tiled=True)
    value_piece = lax.all_gather(value_rows, "seq", axis=0, tiled=True)
    block_rows = math.gcd(key_piece.shape[0], 512)

    def fold_block(inner_state, block_index):
        row_max, row_total, weighted_sum = inner_state
        block_start = block_index * block_rows
        key_block = lax.dynamic_slice_in_dim(key_piece, block_start, block_rows, 0)
        value_block = lax.dynamic_slice_in_dim(value_piece, block_start, block_rows, 0).reshape(
            block_rows, batch_count, HEADS, HEAD
        )
        key_pos = block_start + jnp.arange(block_rows, dtype=jnp.int32)
        scores, allowed = key_block_scores(key_block, key_pos)
        new_max = jnp.maximum(row_max, jnp.max(jnp.where(allowed, scores, neg_large), axis=-1))
        exp_terms = jnp.where(allowed, jnp.exp(scores - new_max[..., None]), 0.0)
        factor = jnp.exp(row_max - new_max)
        row_total = row_total * factor + jnp.sum(exp_terms, axis=-1)
        weighted_sum = weighted_sum * factor[..., None] + jnp.einsum(
            "qbhk,kbhd->qbhd", rounded(exp_terms), value_block, preferred_element_type=jnp.float32
        )
        return ((new_max, row_total, weighted_sum), None)

    running, unused = lax.scan(
        fold_block, running, jnp.arange(key_piece.shape[0] // block_rows, dtype=jnp.int32)
    )
    row_max, row_total, weighted_sum = running
    attended_self = weighted_sum / row_total[..., None]
    log_total = row_max + jnp.log(row_total)
    attended_self_low = rounded(attended_self.reshape(token_count, D))
    middle_rows = (
        input_rows
        + project(attended_self_low, full_self_out)
        + full_self_out_bias.astype(jnp.float32)
    )
    (
        full_cross_gain,
        full_cross_shift,
        full_cross_query,
        full_cross_query_bias,
        full_cross_key,
        full_cross_value,
        full_cross_value_bias,
        full_cross_out,
        full_cross_out_bias,
    ) = (
        lax.all_gather(cross_gain, ("dp", "seq"), axis=0, tiled=True),
        lax.all_gather(cross_shift, ("dp", "seq"), axis=0, tiled=True),
        lax.all_gather(cross_query_weight, ("dp", "seq"), axis=0, tiled=True),
        lax.all_gather(cross_query_bias, ("dp", "seq"), axis=0, tiled=True),
        lax.all_gather(cross_key_weight, ("dp", "seq"), axis=0, tiled=True),
        lax.all_gather(cross_value_weight, ("dp", "seq"), axis=0, tiled=True),
        lax.all_gather(cross_value_bias, ("dp", "seq"), axis=0, tiled=True),
        lax.all_gather(cross_out_weight, ("dp", "seq"), axis=0, tiled=True),
        lax.all_gather(cross_out_bias, ("dp", "seq"), axis=0, tiled=True),
    )
    normed_cross, scaled_cross, inverse_cross = norm_forward(
        middle_rows, full_cross_gain.astype(jnp.float32), full_cross_shift.astype(jnp.float32)
    )
    normed_cross_low = rounded(normed_cross)
    cross_queries = rounded(
        project(normed_cross_low, full_cross_query) + full_cross_query_bias.astype(jnp.float32)
    ).reshape(local_len, batch_count, HEADS, HEAD)
    frame_count = memory.shape[0]
    frame_part = frame_count // seq_count
    frame_start = seq_index * frame_part
    memory_part = lax.dynamic_slice_in_dim(memory, frame_start, frame_part, 0).reshape(
        frame_part * batch_count, D
    )
    memory_flat = memory.reshape(frame_count * batch_count, D)
    memory_keys = rounded(project(memory_flat, full_cross_key)).reshape(frame_count, batch_count, D)
    memory_values = rounded(
        project(memory_flat, full_cross_value) + full_cross_value_bias.astype(jnp.float32)
    ).reshape(frame_count, batch_count, D)
    memory_key_heads = memory_keys.reshape(frame_count, batch_count, HEADS, HEAD)
    memory_value_heads = memory_values.reshape(frame_count, batch_count, HEADS, HEAD)
    frame_valid = (jnp.arange(frame_count, dtype=jnp.int32)[None, :] < memory_lengths[:, None])[
        None, :, None, :
    ]
    cross_scores = (
        jnp.einsum(
            "qbhd,kbhd->qbhk", cross_queries, memory_key_heads, preferred_element_type=jnp.float32
        )
        * 0.125
    )
    cross_max = jnp.max(jnp.where(frame_valid, cross_scores, neg_large), axis=-1, keepdims=True)
    cross_exp = jnp.where(frame_valid, jnp.exp(cross_scores - cross_max), 0.0)
    cross_probs = cross_exp / jnp.sum(cross_exp, axis=-1, keepdims=True)
    cross_probs_low = rounded(cross_probs)
    attended_cross = jnp.einsum(
        "qbhk,kbhd->qbhd", cross_probs_low, memory_value_heads, preferred_element_type=jnp.float32
    )
    attended_cross_low = rounded(attended_cross.reshape(token_count, D))
    after_rows = (
        middle_rows
        + project(attended_cross_low, full_cross_out)
        + full_cross_out_bias.astype(jnp.float32)
    )
    full_mlp_gain, full_mlp_shift, full_fc_in, full_fc_in_bias, full_fc_out, full_fc_out_bias = (
        lax.all_gather(mlp_gain, ("dp", "seq"), axis=0, tiled=True),
        lax.all_gather(mlp_shift, ("dp", "seq"), axis=0, tiled=True),
        lax.all_gather(fc_in_weight, ("dp", "seq"), axis=0, tiled=True),
        lax.all_gather(fc_in_bias, ("dp", "seq"), axis=0, tiled=True),
        lax.all_gather(fc_out_weight, ("dp", "seq"), axis=0, tiled=True),
        lax.all_gather(fc_out_bias, ("dp", "seq"), axis=0, tiled=True),
    )
    normed_mlp, scaled_mlp, inverse_mlp = norm_forward(
        after_rows, full_mlp_gain.astype(jnp.float32), full_mlp_shift.astype(jnp.float32)
    )
    normed_mlp_low = rounded(normed_mlp)
    hidden_pre = project(normed_mlp_low, full_fc_in) + full_fc_in_bias.astype(jnp.float32)
    activated, gelu_pull = jax.vjp(exact_gelu, hidden_pre)
    activated_low = rounded(activated)
    result_rows = (
        after_rows + project(activated_low, full_fc_out) + full_fc_out_bias.astype(jnp.float32)
    )
    output = rounded(result_rows).reshape(local_len, batch_count, D)
    back_fc_in, back_fc_out = (
        lax.all_gather(fc_in_weight, ("dp", "seq"), axis=0, tiled=True),
        lax.all_gather(fc_out_weight, ("dp", "seq"), axis=0, tiled=True),
    )
    grad_result = out_grad.reshape(token_count, D)
    grad_mlp_low = rounded(grad_result)
    grad_fc_out_weight = weight_grad(activated_low, grad_mlp_low)
    grad_fc_out_bias = column_sums(grad_mlp_low)
    grad_activated = project_back(grad_mlp_low, back_fc_out)
    grad_hidden_low = rounded(gelu_pull(grad_activated)[0])
    grad_fc_in_weight = weight_grad(normed_mlp_low, grad_hidden_low)
    grad_fc_in_bias = column_sums(grad_hidden_low)
    grad_normed_mlp = project_back(grad_hidden_low, back_fc_in)
    grad_rows_mlp, grad_mlp_gain, grad_mlp_shift = norm_backward(
        grad_normed_mlp, scaled_mlp, inverse_mlp, full_mlp_gain.astype(jnp.float32)
    )
    grad_after = grad_result + grad_rows_mlp
    back_cross_query, back_cross_key, back_cross_value, back_cross_out = (
        lax.all_gather(cross_query_weight, ("dp", "seq"), axis=0, tiled=True),
        lax.all_gather(cross_key_weight, ("dp", "seq"), axis=0, tiled=True),
        lax.all_gather(cross_value_weight, ("dp", "seq"), axis=0, tiled=True),
        lax.all_gather(cross_out_weight, ("dp", "seq"), axis=0, tiled=True),
    )
    grad_cross_low = rounded(grad_after)
    grad_cross_out_weight = weight_grad(attended_cross_low, grad_cross_low)
    grad_cross_out_bias = column_sums(grad_cross_low)
    grad_attended_cross = rounded(project_back(grad_cross_low, back_cross_out)).reshape(
        local_len, batch_count, HEADS, HEAD
    )
    grad_cross_probs = jnp.einsum(
        "qbhd,kbhd->qbhk",
        grad_attended_cross,
        memory_value_heads,
        preferred_element_type=jnp.float32,
    )
    cross_delta = jnp.sum(cross_probs * grad_cross_probs, axis=-1, keepdims=True)
    grad_cross_scores = rounded(cross_probs * (grad_cross_probs - cross_delta) * 0.125)
    grad_cross_queries = rounded(
        jnp.einsum(
            "qbhk,kbhd->qbhd",
            grad_cross_scores,
            memory_key_heads,
            preferred_element_type=jnp.float32,
        ).reshape(token_count, D)
    )
    grad_memory_keys = jnp.einsum(
        "qbhk,qbhd->kbhd", grad_cross_scores, cross_queries, preferred_element_type=jnp.float32
    ).reshape(frame_count, batch_count, D)
    grad_memory_values = jnp.einsum(
        "qbhk,qbhd->kbhd", cross_probs_low, grad_attended_cross, preferred_element_type=jnp.float32
    ).reshape(frame_count, batch_count, D)
    grad_memory_kv = jnp.concatenate((grad_memory_keys, grad_memory_values), axis=2)
    summed_kv = rounded(lax.psum(grad_memory_kv.astype(jnp.bfloat16), "seq").astype(jnp.float32))
    memory_grad = (
        project_back(summed_kv[:, :, :D].reshape(frame_count * batch_count, D), back_cross_key)
        + project_back(summed_kv[:, :, D:].reshape(frame_count * batch_count, D), back_cross_value)
    ).reshape(frame_count, batch_count, D)
    part_kv = lax.dynamic_slice_in_dim(summed_kv, frame_start, frame_part, 0)
    part_flat_keys = part_kv[:, :, :D].reshape(frame_part * batch_count, D)
    part_flat_values = part_kv[:, :, D:].reshape(frame_part * batch_count, D)
    grad_cross_key_weight = weight_grad(memory_part, part_flat_keys)
    grad_cross_value_weight = weight_grad(memory_part, part_flat_values)
    grad_cross_value_bias = column_sums(part_flat_values)
    grad_cross_query_weight = weight_grad(normed_cross_low, grad_cross_queries)
    grad_cross_query_bias = column_sums(grad_cross_queries)
    grad_normed_cross = project_back(grad_cross_queries, back_cross_query)
    grad_rows_cross, grad_cross_gain, grad_cross_shift = norm_backward(
        grad_normed_cross, scaled_cross, inverse_cross, full_cross_gain.astype(jnp.float32)
    )
    grad_middle = grad_after + grad_rows_cross
    back_query, back_key, back_value, back_self_out = (
        lax.all_gather(query_weight, ("dp", "seq"), axis=0, tiled=True),
        lax.all_gather(key_weight, ("dp", "seq"), axis=0, tiled=True),
        lax.all_gather(value_weight, ("dp", "seq"), axis=0, tiled=True),
        lax.all_gather(attn_out_weight, ("dp", "seq"), axis=0, tiled=True),
    )
    grad_self_low = rounded(grad_middle)
    grad_attn_out_weight = weight_grad(attended_self_low, grad_self_low)
    grad_attn_out_bias = column_sums(grad_self_low)
    grad_attended_self = rounded(project_back(grad_self_low, back_self_out)).reshape(
        local_len, batch_count, HEADS, HEAD
    )
    self_delta = jnp.sum(grad_attended_self.astype(jnp.float32) * attended_self, axis=-1)

    def score_grads(key_block, value_block, key_pos):
        scores, allowed = key_block_scores(key_block, key_pos)
        attn_probs = jnp.where(allowed, jnp.exp(scores - log_total[..., None]), 0.0)
        grad_probs = jnp.einsum(
            "qbhd,kbhd->qbhk", grad_attended_self, value_block, preferred_element_type=jnp.float32
        )
        grad_scores = rounded(attn_probs * (grad_probs - self_delta[..., None]) * 0.125)
        return (grad_scores, attn_probs)

    zero_query_grad = jnp.zeros((local_len, batch_count, HEADS, HEAD), jnp.float32)
    back_state = (zero_query_grad, jnp.zeros((full_length, batch_count, 2 * D), jnp.float32))
    running = back_state
    self_key_piece = lax.all_gather(key_rows, "seq", axis=0, tiled=True)
    self_value_piece = lax.all_gather(value_rows, "seq", axis=0, tiled=True)
    self_block_rows = math.gcd(self_key_piece.shape[0], 512)

    def back_block(inner_state, block_index):
        grad_query_sum, kv_grads = inner_state
        block_start = block_index * self_block_rows
        key_block = lax.dynamic_slice_in_dim(self_key_piece, block_start, self_block_rows, 0)
        value_block = lax.dynamic_slice_in_dim(
            self_value_piece, block_start, self_block_rows, 0
        ).reshape(self_block_rows, batch_count, HEADS, HEAD)
        key_pos = block_start + jnp.arange(self_block_rows, dtype=jnp.int32)
        grad_scores, attn_probs = score_grads(key_block, value_block, key_pos)
        key_heads = key_block.reshape(self_block_rows, batch_count, HEADS, HEAD)
        grad_query_sum = grad_query_sum + jnp.einsum(
            "qbhk,kbhd->qbhd", grad_scores, key_heads, preferred_element_type=jnp.float32
        )
        grad_key_block = jnp.einsum(
            "qbhk,qbhd->kbhd", grad_scores, query_heads, preferred_element_type=jnp.float32
        ).reshape(self_block_rows, batch_count, D)
        grad_value_block = jnp.einsum(
            "qbhk,qbhd->kbhd",
            rounded(attn_probs),
            grad_attended_self,
            preferred_element_type=jnp.float32,
        ).reshape(self_block_rows, batch_count, D)
        kv_grads = lax.dynamic_update_slice_in_dim(
            kv_grads, jnp.concatenate((grad_key_block, grad_value_block), axis=2), block_start, 0
        )
        return ((grad_query_sum, kv_grads), None)

    running, unused = lax.scan(
        back_block, running, jnp.arange(self_key_piece.shape[0] // self_block_rows, dtype=jnp.int32)
    )
    grad_query_sum = running[0]
    own_kv = lax.psum_scatter(
        running[1].astype(jnp.bfloat16), "seq", scatter_dimension=0, tiled=True
    ).astype(jnp.float32)
    grad_key_low = rounded(own_kv[:, :, :D].reshape(token_count, D))
    grad_value_low = rounded(own_kv[:, :, D:].reshape(token_count, D))
    grad_query_low = rounded(grad_query_sum.reshape(token_count, D))
    grad_query_weight = weight_grad(normed_self_low, grad_query_low)
    grad_query_bias = column_sums(grad_query_low)
    grad_key_weight = weight_grad(normed_self_low, grad_key_low)
    grad_value_weight = weight_grad(normed_self_low, grad_value_low)
    grad_value_bias = column_sums(grad_value_low)
    grad_normed_self = (
        project_back(grad_query_low, back_query)
        + project_back(grad_key_low, back_key)
        + project_back(grad_value_low, back_value)
    )
    grad_rows_self, grad_self_gain, grad_self_shift = norm_backward(
        grad_normed_self, scaled_self, inverse_self, full_self_gain.astype(jnp.float32)
    )
    token_grad = (grad_middle + grad_rows_self).reshape(local_len, batch_count, D)
    owned_grads = (
        lax.psum_scatter(grad_self_gain, ("dp", "seq"), scatter_dimension=0, tiled=True),
        lax.psum_scatter(grad_self_shift, ("dp", "seq"), scatter_dimension=0, tiled=True),
        lax.psum_scatter(grad_query_weight, ("dp", "seq"), scatter_dimension=0, tiled=True),
        lax.psum_scatter(grad_query_bias, ("dp", "seq"), scatter_dimension=0, tiled=True),
        lax.psum_scatter(grad_key_weight, ("dp", "seq"), scatter_dimension=0, tiled=True),
        lax.psum_scatter(grad_value_weight, ("dp", "seq"), scatter_dimension=0, tiled=True),
        lax.psum_scatter(grad_value_bias, ("dp", "seq"), scatter_dimension=0, tiled=True),
        lax.psum_scatter(grad_attn_out_weight, ("dp", "seq"), scatter_dimension=0, tiled=True),
        lax.psum_scatter(grad_attn_out_bias, ("dp", "seq"), scatter_dimension=0, tiled=True),
        lax.psum_scatter(grad_cross_gain, ("dp", "seq"), scatter_dimension=0, tiled=True),
        lax.psum_scatter(grad_cross_shift, ("dp", "seq"), scatter_dimension=0, tiled=True),
        lax.psum_scatter(grad_cross_query_weight, ("dp", "seq"), scatter_dimension=0, tiled=True),
        lax.psum_scatter(grad_cross_query_bias, ("dp", "seq"), scatter_dimension=0, tiled=True),
        lax.psum_scatter(grad_cross_key_weight, ("dp", "seq"), scatter_dimension=0, tiled=True),
        lax.psum_scatter(grad_cross_value_weight, ("dp", "seq"), scatter_dimension=0, tiled=True),
        lax.psum_scatter(grad_cross_value_bias, ("dp", "seq"), scatter_dimension=0, tiled=True),
        lax.psum_scatter(grad_cross_out_weight, ("dp", "seq"), scatter_dimension=0, tiled=True),
        lax.psum_scatter(grad_cross_out_bias, ("dp", "seq"), scatter_dimension=0, tiled=True),
        lax.psum_scatter(grad_mlp_gain, ("dp", "seq"), scatter_dimension=0, tiled=True),
        lax.psum_scatter(grad_mlp_shift, ("dp", "seq"), scatter_dimension=0, tiled=True),
        lax.psum_scatter(grad_fc_in_weight, ("dp", "seq"), scatter_dimension=0, tiled=True),
        lax.psum_scatter(grad_fc_in_bias, ("dp", "seq"), scatter_dimension=0, tiled=True),
        lax.psum_scatter(grad_fc_out_weight, ("dp", "seq"), scatter_dimension=0, tiled=True),
        lax.psum_scatter(grad_fc_out_bias, ("dp", "seq"), scatter_dimension=0, tiled=True),
    )
    return (output, token_grad, memory_grad) + tuple(owned_grads)


def solution(mesh):
    in_specs = (
        P("seq", "dp", None),
        P(None, "dp", None),
        P("dp", None),
        P("dp"),
        P(("dp", "seq")),
        P(("dp", "seq")),
        P(("dp", "seq"), None),
        P(("dp", "seq")),
        P(("dp", "seq"), None),
        P(("dp", "seq"), None),
        P(("dp", "seq")),
        P(("dp", "seq"), None),
        P(("dp", "seq")),
        P(("dp", "seq")),
        P(("dp", "seq")),
        P(("dp", "seq"), None),
        P(("dp", "seq")),
        P(("dp", "seq"), None),
        P(("dp", "seq"), None),
        P(("dp", "seq")),
        P(("dp", "seq"), None),
        P(("dp", "seq")),
        P(("dp", "seq")),
        P(("dp", "seq")),
        P(("dp", "seq"), None),
        P(("dp", "seq")),
        P(("dp", "seq"), None),
        P(("dp", "seq")),
        P("seq", "dp", None),
    )
    out_specs = (
        P("seq", "dp", None),
        P("seq", "dp", None),
        P(None, "dp", None),
        P(("dp", "seq")),
        P(("dp", "seq")),
        P(("dp", "seq"), None),
        P(("dp", "seq")),
        P(("dp", "seq"), None),
        P(("dp", "seq"), None),
        P(("dp", "seq")),
        P(("dp", "seq"), None),
        P(("dp", "seq")),
        P(("dp", "seq")),
        P(("dp", "seq")),
        P(("dp", "seq"), None),
        P(("dp", "seq")),
        P(("dp", "seq"), None),
        P(("dp", "seq"), None),
        P(("dp", "seq")),
        P(("dp", "seq"), None),
        P(("dp", "seq")),
        P(("dp", "seq")),
        P(("dp", "seq")),
        P(("dp", "seq"), None),
        P(("dp", "seq")),
        P(("dp", "seq"), None),
        P(("dp", "seq")),
    )
    return jax.shard_map(local, mesh=mesh, in_specs=in_specs, out_specs=out_specs, check_vma=False)
```

profile of v0, /device:TPU:0, one launch (start us, length us, event | category | flops | bytes accessed | tf_op | source)
XLA Modules:
  0.0 2201.4 jit_solution(16905058720225679912)
XLA Ops:
  22.4 43.1 %all-reduce.29 = (bf16[768]{0:T(1024)(128)(2,1)S(1)}, bf16[768]{0:T(1024)(128)(2,1)S(1)}, bf16[768]{0:T(1024)(128)(2,1)S(1)}, bf16[768]{0:T(1024)(128)(2,1)S(1)}...) all-reduce(bf16[768]{0:T(1024)(128)(2,1)S(1)} %dynamic-update-slice, ...), channel_id=1, replica_groups=mesh['dp'=4,'seq'=8] {'dp','seq'}, use_global_device_ids=true, to_apply=%add.1 | all-reduce | flops 13056 | bytes 52224
  70.7 53.1 %all-gather.19.cloned.1.call-done = bf16[768,768]{1,0:T(8,128)(2,1)} async-done(((bf16[24,768]{1,0:T(8,128)(2,1)}), bf16[768,768]{1,0:T(8,128)(2,1)}) %all-gather.19.cloned.1.call-update) | async-done | bytes 1179664 | tf_op jit(solution)/shard_map/all_gather | solution.py:131
  136.0 43.7 %all-gather.17.cloned.1.call-done = bf16[768,768]{1,0:T(8,128)(2,1)} async-done(((bf16[24,768]{1,0:T(8,128)(2,1)}), bf16[768,768]{1,0:T(8,128)(2,1)}) %all-gather.17.cloned.1.call-update) | async-done | bytes 1179664 | tf_op jit(solution)/shard_map/all_gather | solution.py:128
  181.8 53.7 %all-gather.25.cloned.1.call-done = bf16[768,768]{1,0:T(8,128)(2,1)} async-done(((bf16[24,768]{1,0:T(8,128)(2,1)}), bf16[768,768]{1,0:T(8,128)(2,1)}) %all-gather.25.cloned.1.call-update) | async-done | bytes 1179664 | tf_op jit(solution)/shard_map/all_gather | solution.py:210
  235.5 4.7 convolution_convert_fusion
  240.2 51.1 %all-gather.23.cloned.1.call-done = bf16[768,768]{1,0:T(8,128)(2,1)} async-done(((bf16[24,768]{1,0:T(8,128)(2,1)}), bf16[768,768]{1,0:T(8,128)(2,1)}) %all-gather.23.cloned.1.call-update) | async-done | bytes 1179664 | tf_op jit(solution)/shard_map/all_gather | solution.py:211
  291.2 4.7 add_convert_fusion
  296.0 56.8 %all-gather.35.cloned.1.call-done = bf16[2048,768]{1,0:T(8,128)(2,1)} async-done(((bf16[256,768]{1,0:T(8,128)(2,1)}), bf16[2048,768]{1,0:T(8,128)(2,1)}) %all-gather.35.cloned.1.call-update) | async-done | bytes 3145744 | tf_op jit(solution)/shard_map/all_gather | solution.py:161
  352.8 4.9 copy.119
  357.7 56.6 %all-gather.37.cloned.1.call-done = bf16[2048,768]{1,0:T(8,128)(2,1)} async-done(((bf16[256,768]{1,0:T(8,128)(2,1)}), bf16[2048,768]{1,0:T(8,128)(2,1)}) %all-gather.37.cloned.1.call-update) | async-done | bytes 3145744 | tf_op jit(solution)/shard_map/all_gather | solution.py:162
  414.3 4.7 copy.120
  419.0 64.0 %while.28 = (s32[]{:T(128)}, f32[256,1,12]{0,2,1:T(8,128)S(1)}, f32[256,1,12]{0,2,1:T(8,128)S(1)}, f32[256,1,12,64]{0,3,2,1:T(8,128)}, s32[4]{0:T(128)S(1)}, /*i...) while((s32[]{:T(128)}, f32[256,1,12]{0,2,1:T(8,128)S(1)}, ...), condition=%wide.region_7.8_spmd.clone, body=%wide.region_3.7_spmd.clone.sunk | while | flops 421095424 | bytes 51460936 | solution.py:183
  422.9 3.8 fusion.226
  426.8 4.2 fusion.228
  438.7 3.8 fusion.226
  442.6 4.2 fusion.228
  454.8 3.8 fusion.226
  458.7 4.2 fusion.228
  470.9 3.8 fusion.226
  474.8 4.2 fusion.228
  479.4 3.6 fusion.229
  488.6 37.2 %all-gather.27.cloned.1.call-done = bf16[768,768]{1,0:T(8,128)(2,1)} async-done(((bf16[24,768]{1,0:T(8,128)(2,1)}), bf16[768,768]{1,0:T(8,128)(2,1)}) %all-gather.27.cloned.1.call-update) | async-done | bytes 1179664 | tf_op jit(solution)/shard_map/all_gather | solution.py:208
  530.4 6.0 fusion.53
  536.5 5.2 fusion.57
  543.6 4.7 fusion.83
  548.3 33.3 %all-gather.29.cloned.1.call-done = bf16[768,768]{1,0:T(8,128)(2,1)} async-done(((bf16[24,768]{1,0:T(8,128)(2,1)}), bf16[768,768]{1,0:T(8,128)(2,1)}) %all-gather.29.cloned.1.call-update) | async-done | bytes 1179664 | tf_op jit(solution)/shard_map/all_gather | solution.py:213
  585.3 61.7 %all-gather.31.cloned.1.call-done = bf16[768,3072]{1,0:T(8,128)(2,1)} async-done(((bf16[24,3072]{1,0:T(8,128)(2,1)}), bf16[768,3072]{1,0:T(8,128)(2,1)}) %all-gather.31.cloned.1.call-update) | async-done | bytes 4718608 | tf_op jit(solution)/shard_map/all_gather | solution.py:261
  647.0 12.0 multiply_convert_fusion
  659.0 52.7 %all-gather.33.cloned.1.call-done = bf16[3072,768]{1,0:T(8,128)(2,1)} async-done(((bf16[96,768]{1,0:T(8,128)(2,1)}), bf16[3072,768]{1,0:T(8,128)(2,1)}) %all-gather.33.cloned.1.call-update) | async-done | bytes 4718608 | tf_op jit(solution)/shard_map/all_gather | solution.py:263
  711.7 7.0 convert_reduce_fusion
  724.3 15.5 fusion.49
  739.8 10.5 fusion.64
  750.3 10.8 fusion.58
  767.1 8.2 convolution_convert_fusion.1
  781.6 4.9 pad_maximum_fusion
  790.1 74.4 %while.29 = (s32[]{:T(128)}, f32[256,1,12,64]{0,3,2,1:T(8,128)}, bf16[2048,1,1536]{0,2,1:T(8,128)(2,1)}, s32[4]{0:T(128)S(1)}, bf16[2048,1,768]{0,2,1:T(8,128)(2...) while((s32[]{:T(128)}, f32[256,1,12,64]{0,3,2,1:T(8,128)}, ...), condition=%wide.region_22.23_spmd.clone, body=%wide.region_20.22_spmd.clone.sunk | while | flops 1028005888 | bytes 84216896 | solution.py:404
  794.7 3.9 fusion.242
  802.2 4.4 fusion.244
  813.1 3.9 fusion.242
  817.0 3.7 fusion.243
  820.7 4.3 fusion.244
  831.7 3.9 fusion.242
  835.6 3.7 fusion.243
  839.3 4.3 fusion.244
  850.2 3.9 fusion.242
  854.1 3.7 fusion.243
  857.8 4.3 fusion.244
  879.1 75.4 %all-reduce.32.cloned.1.call-done = bf16[1536,1,1536]{0,2,1:T(8,128)(2,1)} async-done(((bf16[1536,1,1536]{0,2,1:T(8,128)(2,1)}), bf16[1536,1,1536]{0,2,1:T(8,128)(2,1)}) %all-reduce.32.cloned.1.call-update) | async-done | bytes 4718608 | tf_op jit(solution)/shard_map/psum | solution.py:329
  961.2 6.6 fusion.135
  968.1 6.7 fusion.132
  974.8 100.6 %reduce-scatter.12.cloned.1.call-done = bf16[256,1,1536]{0,2,1:T(8,128)(2,1)} async-done(((bf16[2048,1,1536]{0,2,1:T(8,128)(2,1)}), bf16[256,1,1536]{0,2,1:T(8,128)(2,1)}) %reduce-scatter.12.cloned.1.call-update) | async-done | bytes 786448 | tf_op jit(solution)/shard_map/reduce_scatter | solution.py:408
  1088.6 5.2 fusion.86
  1093.8 3.9 fusion.73
  1099.8 26.7 %copy.131 = f32[1536,1,768]{2,1,0:T(1,128)} copy(f32[1536,1,768]{2,0,1:T(8,128)S(1)} %add_bitcast_fusion) | data formatting | bytes 9437184
  1131.0 41.2 %all-reduce.28 = (f32[768]{0:T(1024)S(1)}, f32[768]{0:T(1024)S(1)}, f32[768]{0:T(1024)S(1)}, f32[768]{0:T(1024)S(1)}, f32[768]{0:T(1024)S(1)}, /*index=5*/f32[76...) all-reduce(f32[768]{0:T(1024)S(1)} %get-tuple-element.451, ...), channel_id=5, replica_groups=mesh['dp'=4,'seq'=8] {'dp','seq'}, use_global_device_ids=true, to_apply=%region_28.29.clone | all-reduce | flops 13056 | bytes 104448
  1180.3 104.2 %reduce-scatter.20.cloned.1.call-done = f32[24,768]{1,0:T(8,128)} async-done(((f32[768,768]{1,0:T(8,128)}), f32[24,768]{1,0:T(8,128)}) %reduce-scatter.20.cloned.1.call-update) | async-done | bytes 73744 | tf_op jit(solution)/shard_map/reduce_scatter | solution.py:436
  1284.5 104.4 %reduce-scatter.22.cloned.1.call-done = f32[24,768]{1,0:T(8,128)} async-done(((f32[768,768]{1,0:T(8,128)}), f32[24,768]{1,0:T(8,128)}) %reduce-scatter.22.cloned.1.call-update) | async-done | bytes 73744 | tf_op jit(solution)/shard_map/reduce_scatter | solution.py:440
  1388.9 104.4 %reduce-scatter.28.cloned.1.call-done = f32[24,768]{1,0:T(8,128)} async-done(((f32[768,768]{1,0:T(8,128)}), f32[24,768]{1,0:T(8,128)}) %reduce-scatter.28.cloned.1.call-update) | async-done | bytes 73744 | tf_op jit(solution)/shard_map/reduce_scatter | solution.py:445
  1493.3 104.5 %reduce-scatter.24.cloned.1.call-done = f32[24,768]{1,0:T(8,128)} async-done(((f32[768,768]{1,0:T(8,128)}), f32[24,768]{1,0:T(8,128)}) %reduce-scatter.24.cloned.1.call-update) | async-done | bytes 73744 | tf_op jit(solution)/shard_map/reduce_scatter | solution.py:442
  1597.8 104.3 %reduce-scatter.26.cloned.1.call-done = f32[24,768]{1,0:T(8,128)} async-done(((f32[768,768]{1,0:T(8,128)}), f32[24,768]{1,0:T(8,128)}) %reduce-scatter.26.cloned.1.call-update) | async-done | bytes 73744 | tf_op jit(solution)/shard_map/reduce_scatter | solution.py:443
  1702.1 141.7 %reduce-scatter.30.cloned.1.call-done = f32[24,3072]{1,0:T(8,128)} async-done(((f32[768,3072]{1,0:T(8,128)}), f32[24,3072]{1,0:T(8,128)}) %reduce-scatter.30.cloned.1.call-update) | async-done | bytes 294928 | tf_op jit(solution)/shard_map/reduce_scatter | solution.py:449
  1843.8 141.7 %reduce-scatter.32.cloned.1.call-done = f32[96,768]{1,0:T(8,128)} async-done(((f32[3072,768]{1,0:T(8,128)}), f32[96,768]{1,0:T(8,128)}) %reduce-scatter.32.cloned.1.call-update) | async-done | bytes 294928 | tf_op jit(solution)/shard_map/reduce_scatter | solution.py:451
  1985.5 104.5 %reduce-scatter.16.cloned.1.call-done = f32[24,768]{1,0:T(8,128)} async-done(((f32[768,768]{1,0:T(8,128)}), f32[24,768]{1,0:T(8,128)}) %reduce-scatter.16.cloned.1.call-update) | async-done | bytes 73744 | tf_op jit(solution)/shard_map/reduce_scatter | solution.py:433
  2090.0 104.4 %reduce-scatter.18.cloned.1.call-done = f32[24,768]{1,0:T(8,128)} async-done(((f32[768,768]{1,0:T(8,128)}), f32[24,768]{1,0:T(8,128)}) %reduce-scatter.18.cloned.1.call-update) | async-done | bytes 73744 | tf_op jit(solution)/shard_map/reduce_scatter | solution.py:434
  (523 shorter events, 171.7 us)
Async XLA Ops:
  7.2 228.3 %copy-start = (bf16[1536,1,768]{2,0,1:T(8,128)(2,1)S(1)}, bf16[1536,1,768]{2,0,1:T(8,128)(2,1)}, u32[]{:S(2)}) copy-start(bf16[1536,1,768]{2,0,1:T(8,128)(2,1)} %param.34) | copy-start | bytes 7077892
  7.2 116.6 %copy-start.13 = (bf16[256,1,768]{2,0,1:T(8,128)(2,1)S(1)}, bf16[256,1,768]{2,0,1:T(8,128)(2,1)}, u32[]{:S(2)}) copy-start(bf16[256,1,768]{2,0,1:T(8,128)(2,1)} %param.33) | copy-start | bytes 1179652
  7.2 60.7 %all-gather.15.cloned.1.call-start = ((), (), s32[]{:S(2)}) async-start(), calls=%async_computation.11 | async-start | bytes 1216512 | tf_op jit(solution)/shard_map/all_gather | solution.py:130
  8.0 115.9 %all-gather.19.cloned.1.call-start = ((), (), s32[]{:S(2)}) async-start(), calls=%async_computation.13 | async-start | bytes 1216512 | tf_op jit(solution)/shard_map/all_gather | solution.py:131
  8.7 171.0 %all-gather.17.cloned.1.call-start = ((), (), s32[]{:S(2)}) async-start(), calls=%async_computation.12 | async-start | bytes 1216512 | tf_op jit(solution)/shard_map/all_gather | solution.py:128
  9.4 226.0 %all-gather.25.cloned.1.call-start = ((), (), s32[]{:S(2)}) async-start(), calls=%async_computation.16 | async-start | bytes 1216512 | tf_op jit(solution)/shard_map/all_gather | solution.py:210
  10.0 281.2 %all-gather.23.cloned.1.call-start = ((), (), s32[]{:S(2)}) async-start(), calls=%async_computation.15 | async-start | bytes 1216512 | tf_op jit(solution)/shard_map/all_gather | solution.py:211
  10.6 342.2 %all-gather.35.cloned.1.call-start = ((), (), s32[]{:S(2)}) async-start(), calls=%async_computation.33 | async-start | bytes 3538944 | tf_op jit(solution)/shard_map/all_gather | solution.py:161
  65.5 114.2 %copy-start.52 = (f32[768]{0:T(1024)}, f32[768]{0:T(1024)S(1)}, u32[]{:S(2)}) copy-start(f32[768]{0:T(1024)S(1)} %convert_element_type.241) | copy-start | bytes 9220
  65.5 114.2 %copy-start.47 = (f32[768]{0:T(1024)}, f32[768]{0:T(1024)S(1)}, u32[]{:S(2)}) copy-start(f32[768]{0:T(1024)S(1)} %convert_element_type.240) | copy-start | bytes 9220
  66.7 113.1 %copy-start.58 = (f32[256]{0:T(256)}, f32[256]{0:T(256)S(1)}, u32[]{:S(2)}) copy-start(f32[256]{0:T(256)S(1)} %broadcast_multiply_fusion.8) | copy-start | bytes 3076
  67.9 111.8 %copy-start.63 = (f32[256]{0:T(256)}, f32[256]{0:T(256)S(1)}, u32[]{:S(2)}) copy-start(f32[256]{0:T(256)S(1)} %add_rsqrt_fusion.2) | copy-start | bytes 3076
  67.9 63.2 %copy-start.54 = (s32[1,3]{1,0:T(1,128)S(1)}, s32[1,3]{1,0:T(1,128)}, u32[]{:S(2)}) copy-start(s32[1,3]{1,0:T(1,128)} %param.35) | copy-start | bytes 40
  70.7 343.6 %all-gather.37.cloned.1.call-start = ((), (), s32[]{:S(2)}) async-start(), calls=%async_computation.34 | async-start | bytes 3538944 | tf_op jit(solution)/shard_map/all_gather | solution.py:162
  126.4 358.7 %all-gather.21.cloned.1.call-start = ((), (), s32[]{:S(2)}) async-start(), calls=%async_computation.14 | async-start | bytes 1216512 | tf_op jit(solution)/shard_map/all_gather | solution.py:133
  127.2 398.7 %all-gather.27.cloned.1.call-start = ((), (), s32[]{:S(2)}) async-start(), calls=%async_computation.17 | async-start | bytes 1216512 | tf_op jit(solution)/shard_map/all_gather | solution.py:208
  127.9 453.7 %all-gather.29.cloned.1.call-start = ((), (), s32[]{:S(2)}) async-start(), calls=%async_computation.18 | async-start | bytes 1216512 | tf_op jit(solution)/shard_map/all_gather | solution.py:213
  128.5 518.5 %all-gather.31.cloned.1.call-start = ((), (), s32[]{:S(2)}) async-start(), calls=%async_computation.19 | async-start | bytes 4866048 | tf_op jit(solution)/shard_map/all_gather | solution.py:261
  129.2 582.5 %all-gather.33.cloned.1.call-start = ((), (), s32[]{:S(2)}) async-start(), calls=%async_computation.20 | async-start | bytes 4866048 | tf_op jit(solution)/shard_map/all_gather | solution.py:263
  129.8 824.7 %all-reduce.32.cloned.1.call-start = ((), (), s32[]{:S(2)}) async-start(), calls=%async_computation.22 | async-start | bytes 9437184 | tf_op jit(solution)/shard_map/psum | solution.py:329
  458.6 4.6 copy-start.1
  483.0 45.5 %copy-start.6 = (bf16[256,1,12,64]{0,3,2,1:T(8,128)(2,1)}, bf16[256,1,12,64]{0,3,2,1:T(8,128)(2,1)S(1)}, u32[]{:S(2)}) copy-start(bf16[256,1,12,64]{0,3,2,1:T(8,128)(2,1)S(1)} %get-tuple-element.864) | copy-start | bytes 1179652
  487.2 94.4 %copy-start.10 = (f32[256,768]{1,0:T(8,128)}, f32[256,768]{1,0:T(8,128)S(1)}, u32[]{:S(2)}) copy-start(f32[256,768]{1,0:T(8,128)S(1)} %get-tuple-element.557) | copy-start | bytes 2359300
  530.4 6.1 copy-start.56
  536.5 7.1 copy-start.3
  536.5 7.1 copy-start.41
  536.5 7.1 copy-start.90
  548.3 36.3 %copy-start.35 = (bf16[12,64,256]{2,1,0:T(8,128)(2,1)}, bf16[12,64,256]{2,1,0:T(8,128)(2,1)S(1)}, u32[]{:S(2)}) copy-start(bf16[12,64,256]{2,1,0:T(8,128)(2,1)S(1)} %fusion.83) | copy-start | bytes 1179652
  583.5 137.4 %copy-start.66 = (f32[256]{0:T(256)}, f32[256]{0:T(256)S(1)}, u32[]{:S(2)}) copy-start(f32[256]{0:T(256)S(1)} %broadcast_multiply_fusion.6) | copy-start | bytes 3076
  584.6 136.3 %copy-start.78 = (f32[256]{0:T(256)}, f32[256]{0:T(256)S(1)}, u32[]{:S(2)}) copy-start(f32[256]{0:T(256)S(1)} %add_rsqrt_fusion) | copy-start | bytes 3076
  585.3 126.4 %copy-start.32 = (f32[256,1,768]{2,1,0:T(1,128)S(1)}, f32[256,1,768]{2,1,0:T(1,128)}, u32[]{:S(2)}) copy-start(f32[256,1,768]{2,1,0:T(1,128)} %param.61) | copy-start | bytes 2359300
  711.7 7.0 copy-start.20
  711.7 7.0 copy-start.43
  711.7 7.0 copy-start.85
  724.2 26.0 %slice-start = ((s8[18874368]{0:T(1024)(128)(4,1)}), s8[4194304]{0:T(1024)(128)(4,1)S(1)}, s32[]{:S(2)}) async-start(s8[18874368]{0:T(1024)(128)(4,1)} %bitcast.443), calls=%async_computation.35 | async-start | bytes 8388608
  724.3 26.0 %slice-start.1 = ((s8[18874368]{0:T(1024)(128)(4,1)}), s8[4194304]{0:T(1024)(128)(4,1)S(1)}, s32[]{:S(2)}) async-start(s8[18874368]{0:T(1024)(128)(4,1)} %bitcast.443), calls=%async_computation.36 | async-start | bytes 8388608
  724.3 26.0 %slice-start.2 = ((s8[18874368]{0:T(1024)(128)(4,1)}), s8[2097152]{0:T(1024)(128)(4,1)S(1)}, s32[]{:S(2)}) async-start(s8[18874368]{0:T(1024)(128)(4,1)} %bitcast.443), calls=%async_computation.37 | async-start | bytes 4194304
  739.8 10.5 slice-start.3
  739.8 10.5 slice-start.4
  750.3 14.4 copy-start.9
  767.1 8.2 copy-start.31
  767.1 8.2 copy-start.11
  767.1 8.2 copy-start.61
  767.1 8.2 copy-start.69
  767.1 8.2 copy-start.80
  767.1 8.2 copy-start.89
  786.5 288.9 %reduce-scatter.12.cloned.1.call-start = ((), (), s32[]{:S(2)}) async-start(), calls=%async_computation.21 | async-start | bytes 7077888 | tf_op jit(solution)/shard_map/reduce_scatter | solution.py:408
  864.6 315.8 %reduce-scatter.14.cloned.1.call-start = ((), (), s32[]{:S(2)}) async-start(), calls=%async_computation.23 | async-start | bytes 2433024 | tf_op jit(solution)/shard_map/reduce_scatter | solution.py:431
  869.3 415.2 %reduce-scatter.20.cloned.1.call-start = ((), (), s32[]{:S(2)}) async-start(), calls=%async_computation.26 | async-start | bytes 2433024 | tf_op jit(solution)/shard_map/reduce_scatter | solution.py:436
  872.6 516.3 %reduce-scatter.22.cloned.1.call-start = ((), (), s32[]{:S(2)}) async-start(), calls=%async_computation.27 | async-start | bytes 2433024 | tf_op jit(solution)/shard_map/reduce_scatter | solution.py:440
  875.8 617.5 %reduce-scatter.28.cloned.1.call-start = ((), (), s32[]{:S(2)}) async-start(), calls=%async_computation.30 | async-start | bytes 2433024 | tf_op jit(solution)/shard_map/reduce_scatter | solution.py:445
  879.0 718.8 %reduce-scatter.24.cloned.1.call-start = ((), (), s32[]{:S(2)}) async-start(), calls=%async_computation.28 | async-start | bytes 2433024 | tf_op jit(solution)/shard_map/reduce_scatter | solution.py:442
  957.8 744.3 %reduce-scatter.26.cloned.1.call-start = ((), (), s32[]{:S(2)}) async-start(), calls=%async_computation.29 | async-start | bytes 2433024 | tf_op jit(solution)/shard_map/reduce_scatter | solution.py:443
  961.1 882.7 %reduce-scatter.30.cloned.1.call-start = ((), (), s32[]{:S(2)}) async-start(), calls=%async_computation.31 | async-start | bytes 9732096 | tf_op jit(solution)/shard_map/reduce_scatter | solution.py:449
  967.8 1017.7 %reduce-scatter.32.cloned.1.call-start = ((), (), s32[]{:S(2)}) async-start(), calls=%async_computation.32 | async-start | bytes 9732096 | tf_op jit(solution)/shard_map/reduce_scatter | solution.py:451
  974.8 100.7 %copy-start.60 = (f32[256]{0:T(256)S(1)}, f32[256]{0:T(256)}, u32[]{:S(2)}) copy-start(f32[256]{0:T(256)} %copy-done.58) | copy-start | bytes 3076
  974.8 100.7 %copy-start.65 = (f32[256]{0:T(256)S(1)}, f32[256]{0:T(256)}, u32[]{:S(2)}) copy-start(f32[256]{0:T(256)} %copy-done.63) | copy-start | bytes 3076
  974.8 1115.2 %reduce-scatter.16.cloned.1.call-start = ((), (), s32[]{:S(2)}) async-start(), calls=%async_computation.24 | async-start | bytes 2433024 | tf_op jit(solution)/shard_map/reduce_scatter | solution.py:433
  1078.6 1115.7 %reduce-scatter.18.cloned.1.call-start = ((), (), s32[]{:S(2)}) async-start(), calls=%async_computation.25 | async-start | bytes 2433024 | tf_op jit(solution)/shard_map/reduce_scatter | solution.py:434
  1088.6 5.2 copy-start.87
  1088.6 9.1 slice-start.5
  1099.8 27.1 %copy-start.29 = (bf16[256,1,1536]{0,2,1:T(8,128)(2,1)S(1)}, bf16[256,1,1536]{0,2,1:T(8,128)(2,1)}, u32[]{:S(2)}) copy-start(bf16[256,1,1536]{0,2,1:T(8,128)(2,1)} %reduce-scatter.12.cloned.1.call-done) | copy-start | bytes 2359300
  1099.8 27.1 %copy-start.30 = (f32[256,768]{1,0:T(8,128)S(1)}, f32[256,768]{1,0:T(8,128)}, u32[]{:S(2)}) copy-start(f32[256,768]{1,0:T(8,128)} %fusion.148) | copy-start | bytes 2359300
  1099.8 27.1 %copy-start.37 = (bf16[768,768]{1,0:T(8,128)(2,1)S(1)}, bf16[768,768]{1,0:T(8,128)(2,1)}, u32[]{:S(2)}) copy-start(bf16[768,768]{1,0:T(8,128)(2,1)} %all-gather.15.cloned.1.call-done) | copy-start | bytes 3538948
  (88 other events, 248.9 us)
Sparse Core Ops, SparseCore 0:
  10.9 56.7 all-gather.14
  70.7 53.0 all-gather.18
  126.8 52.9 all-gather.16
  182.5 52.9 all-gather.24
  238.3 52.9 all-gather.22
  293.9 58.9 all-gather.34
  355.6 58.6 all-gather.36
  417.2 52.7 all-gather.20
  472.9 52.9 all-gather.26
  528.6 52.9 all-gather.28
  584.5 62.3 all-gather.30
  649.7 61.8 all-gather.32
  786.7 167.8 all-reduce.31
  958.0 117.4 reduce-scatter.11
  1081.2 98.9 reduce-scatter.13
  1185.9 98.5 reduce-scatter.19
  1290.2 98.6 reduce-scatter.21
  1394.6 98.6 reduce-scatter.27
  1499.1 98.6 reduce-scatter.23
  1603.5 98.5 reduce-scatter.25
  1708.6 135.1 reduce-scatter.29
  1850.3 135.1 reduce-scatter.31
  1991.4 98.5 reduce-scatter.15
  2095.7 98.6 reduce-scatter.17
where the time goes:
time: 2210 us; the launch traced here: 2200 us
  waiting for transfers between devices  1700 us (77%)
  matrix products  232 us (10%)
  local copies, waits for them, and re-layouts  101 us (5%)
  blocking collectives  84.3 us (4%)
  other arithmetic  63.7 us (3%)
    reduce_scatter x1, waiting for transfers between devices, local(): lax.psum_scatter(grad_fc_in_weight, ('dp', 'seq'), scatter_dimension=0, t...  142 us
    reduce_scatter x1, waiting for transfers between devices, local(): lax.psum_scatter(grad_fc_out_weight, ('dp', 'seq'), scatter_dimension=0,...  142 us
    reduce_scatter x1, waiting for transfers between devices, local(): lax.psum_scatter(grad_cross_key_weight, ('dp', 'seq'), scatter_dimension=...  105 us
    reduce_scatter x1, waiting for transfers between devices, local(): lax.psum_scatter(grad_key_weight, ('dp', 'seq'), scatter_dimension=0, til...  104 us
    reduce_scatter x1, waiting for transfers between devices, local(): lax.psum_scatter(grad_cross_out_weight, ('dp', 'seq'), scatter_dimension=...  104 us
    reduce_scatter x1, waiting for transfers between devices, local(): lax.psum_scatter(grad_value_weight, ('dp', 'seq'), scatter_dimension=0, t...  104 us
    reduce_scatter x1, waiting for transfers between devices, local(): lax.psum_scatter(grad_cross_query_weight, ('dp', 'seq'), scatter_dimensio...  104 us
    reduce_scatter x1, waiting for transfers between devices, local(): lax.psum_scatter(grad_cross_value_weight, ('dp', 'seq'), scatter_dimensio...  104 us
  transfers between devices with their start and end apart: 24, of which 21 were waited for; matrix products, arithmetic and copies ran while one was open for 14% of the time, Pallas kernels for 0%

commit v1 on v0

--- a/solution.py
+++ b/solution.py
@@ -112,27 +112,87 @@
     query_pos = seq_index * local_len + jnp.arange(local_len, dtype=jnp.int32)
     query_label = piece_labels(query_pos, piece_starts)
     input_rows = tokens.reshape(token_count, D).astype(jnp.float32)
+    shard_rows = query_weight.shape[0]
+    wide_parts = fc_in_weight.shape[1] // D
+    vectors = jnp.concatenate(
+        (
+            self_gain,
+            self_shift,
+            query_bias,
+            value_bias,
+            attn_out_bias,
+            cross_gain,
+            cross_shift,
+            cross_query_bias,
+            cross_value_bias,
+            cross_out_bias,
+            mlp_gain,
+            mlp_shift,
+            fc_out_bias,
+            fc_in_bias,
+        )
+    )
+    vector_rows = 8
+    vector_block = jnp.pad(vectors, (0, vector_rows * D - vectors.shape[0])).reshape(vector_rows, D)
+    fc_in_blocks = jnp.transpose(
+        fc_in_weight.reshape(shard_rows, wide_parts, D), (1, 0, 2)
+    ).reshape(wide_parts * shard_rows, D)
+    packed = jnp.concatenate(
+        (
+            query_weight,
+            key_weight,
+            value_weight,
+            attn_out_weight,
+            cross_query_weight,
+            cross_key_weight,
+            cross_value_weight,
+            cross_out_weight,
+            fc_in_blocks,
+            fc_out_weight,
+            vector_block,
+        )
+    )
+    gathered = lax.all_gather(packed, ("dp", "seq"), axis=0, tiled=False)
+    owners = gathered.shape[0]
+
+    def square_at(slot):
+        return gathered[:, slot * shard_rows : (slot + 1) * shard_rows, :].reshape(D, D)
+
+    full_query, full_key, full_value, full_self_out = (square_at(slot) for slot in range(4))
+    full_cross_query, full_cross_key, full_cross_value, full_cross_out = (
+        square_at(slot) for slot in range(4, 8)
+    )
+    wide_start = 8 * shard_rows
+    wide_stop = wide_start + wide_parts * shard_rows
+    full_fc_in = jnp.transpose(
+        gathered[:, wide_start:wide_stop, :].reshape(owners, wide_parts, shard_rows, D),
+        (0, 2, 1, 3),
+    ).reshape(D, wide_parts * D)
+    out_stop = wide_stop + fc_out_weight.shape[0]
+    full_fc_out = gathered[:, wide_stop:out_stop, :].reshape(wide_parts * D, D)
+    full_vectors = gathered[:, out_stop:, :].reshape(owners, vector_rows * D)
+
+    def vector_at(slot):
+        return full_vectors[:, slot * shard_rows : (slot + 1) * shard_rows].reshape(D)
+
     (
         full_self_gain,
         full_self_shift,
-        full_query,
         full_query_bias,
-        full_key,
-        full_value,
         full_value_bias,
-        full_self_out,
         full_self_out_bias,
-    ) = (
-        lax.all_gather(self_gain, ("dp", "seq"), axis=0, tiled=True),
-        lax.all_gather(self_shift, ("dp", "seq"), axis=0, tiled=True),
-        lax.all_gather(query_weight, ("dp", "seq"), axis=0, tiled=True),
-        lax.all_gather(query_bias, ("dp", "seq"), axis=0, tiled=True),
-        lax.all_gather(key_weight, ("dp", "seq"), axis=0, tiled=True),
-        lax.all_gather(value_weight, ("dp", "seq"), axis=0, tiled=True),
-        lax.all_gather(value_bias, ("dp", "seq"), axis=0, tiled=True),
-        lax.all_gather(attn_out_weight, ("dp", "seq"), axis=0, tiled=True),
-        lax.all_gather(attn_out_bias, ("dp", "seq"), axis=0, tiled=True),
-    )
+        full_cross_gain,
+        full_cross_shift,
+        full_cross_query_bias,
+        full_cross_value_bias,
+        full_cross_out_bias,
+        full_mlp_gain,
+        full_mlp_shift,
+        full_fc_out_bias,
+    ) = (vector_at(slot) for slot in range(13))
+    full_fc_in_bias = full_vectors[
+        :, 13 * shard_rows : 13 * shard_rows + fc_in_bias.shape[0]
+    ].reshape(-1)
     normed_self, scaled_self, inverse_self = norm_forward(
         input_rows, full_self_gain.astype(jnp.float32), full_self_shift.astype(jnp.float32)
     )
@@ -158,8 +218,11 @@
         jnp.zeros((local_len, batch_count, HEADS, HEAD), jnp.float32),
     )
     running = start_state
-    key_piece = lax.all_gather(key_rows, "seq", axis=0, tiled=True)
-    value_piece = lax.all_gather(value_rows, "seq", axis=0, tiled=True)
+    kv_piece = lax.all_gather(
+        jnp.concatenate((key_rows, value_rows), axis=2), "seq", axis=0, tiled=True
+    )
+    key_piece = kv_piece[:, :, :D]
+    value_piece = kv_piece[:, :, D:]
     block_rows = math.gcd(key_piece.shape[0], 512)
 
     def fold_block(inner_state, block_index):
@@ -191,27 +254,6 @@
         input_rows
         + project(attended_self_low, full_self_out)
         + full_self_out_bias.astype(jnp.float32)
-    )
-    (
-        full_cross_gain,
-        full_cross_shift,
-        full_cross_query,
-        full_cross_query_bias,
-        full_cross_key,
-        full_cross_value,
-        full_cross_value_bias,
-        full_cross_out,
-        full_cross_out_bias,
-    ) = (
-        lax.all_gather(cross_gain, ("dp", "seq"), axis=0, tiled=True),
-        lax.all_gather(cross_shift, ("dp", "seq"), axis=0, tiled=True),
-        lax.all_gather(cross_query_weight, ("dp", "seq"), axis=0, tiled=True),
-        lax.all_gather(cross_query_bias, ("dp", "seq"), axis=0, tiled=True),
-        lax.all_gather(cross_key_weight, ("dp", "seq"), axis=0, tiled=True),
-        lax.all_gather(cross_value_weight, ("dp", "seq"), axis=0, tiled=True),
-        lax.all_gather(cross_value_bias, ("dp", "seq"), axis=0, tiled=True),
-        lax.all_gather(cross_out_weight, ("dp", "seq"), axis=0, tiled=True),
-        lax.all_gather(cross_out_bias, ("dp", "seq"), axis=0, tiled=True),
     )
     normed_cross, scaled_cross, inverse_cross = norm_forward(
         middle_rows, full_cross_gain.astype(jnp.float32), full_cross_shift.astype(jnp.float32)
@@ -255,14 +297,6 @@
         + project(attended_cross_low, full_cross_out)
         + full_cross_out_bias.astype(jnp.float32)
     )
-    full_mlp_gain, full_mlp_shift, full_fc_in, full_fc_in_bias, full_fc_out, full_fc_out_bias = (
-        lax.all_gather(mlp_gain, ("dp", "seq"), axis=0, tiled=True),
-        lax.all_gather(mlp_shift, ("dp", "seq"), axis=0, tiled=True),
-        lax.all_gather(fc_in_weight, ("dp", "seq"), axis=0, tiled=True),
-        lax.all_gather(fc_in_bias, ("dp", "seq"), axis=0, tiled=True),
-        lax.all_gather(fc_out_weight, ("dp", "seq"), axis=0, tiled=True),
-        lax.all_gather(fc_out_bias, ("dp", "seq"), axis=0, tiled=True),
-    )
     normed_mlp, scaled_mlp, inverse_mlp = norm_forward(
         after_rows, full_mlp_gain.astype(jnp.float32), full_mlp_shift.astype(jnp.float32)
     )
@@ -274,10 +308,7 @@
         after_rows + project(activated_low, full_fc_out) + full_fc_out_bias.astype(jnp.float32)
     )
     output = rounded(result_rows).reshape(local_len, batch_count, D)
-    back_fc_in, back_fc_out = (
-        lax.all_gather(fc_in_weight, ("dp", "seq"), axis=0, tiled=True),
-        lax.all_gather(fc_out_weight, ("dp", "seq"), axis=0, tiled=True),
-    )
+    back_fc_in, back_fc_out = full_fc_in, full_fc_out
     grad_result = out_grad.reshape(token_count, D)
     grad_mlp_low = rounded(grad_result)
     grad_fc_out_weight = weight_grad(activated_low, grad_mlp_low)
@@ -290,12 +321,32 @@
     grad_rows_mlp, grad_mlp_gain, grad_mlp_shift = norm_backward(
         grad_normed_mlp, scaled_mlp, inverse_mlp, full_mlp_gain.astype(jnp.float32)
     )
+    early_grads = jnp.concatenate(
+        (
+            jnp.transpose(
+                grad_fc_in_weight.astype(jnp.bfloat16).reshape(
+                    owners, shard_rows, wide_parts, D
+                ),
+                (0, 2, 1, 3),
+            ).reshape(owners, wide_parts * shard_rows, D),
+            grad_fc_out_weight.astype(jnp.bfloat16).reshape(owners, -1, D),
+        ),
+        axis=1,
+    )
+    owned_early = lax.psum_scatter(
+        early_grads, ("dp", "seq"), scatter_dimension=0, tiled=False
+    ).astype(jnp.float32)
+    wide_rows = wide_parts * shard_rows
+    owned_fc_in = jnp.transpose(
+        owned_early[:wide_rows].reshape(wide_parts, shard_rows, D), (1, 0, 2)
+    ).reshape(shard_rows, wide_parts * D)
+    owned_fc_out = owned_early[wide_rows:]
     grad_after = grad_result + grad_rows_mlp
     back_cross_query, back_cross_key, back_cross_value, back_cross_out = (
-        lax.all_gather(cross_query_weight, ("dp", "seq"), axis=0, tiled=True),
-        lax.all_gather(cross_key_weight, ("dp", "seq"), axis=0, tiled=True),
-        lax.all_gather(cross_value_weight, ("dp", "seq"), axis=0, tiled=True),
-        lax.all_gather(cross_out_weight, ("dp", "seq"), axis=0, tiled=True),
+        full_cross_query,
+        full_cross_key,
+        full_cross_value,
+        full_cross_out,
     )
     grad_cross_low = rounded(grad_after)
     grad_cross_out_weight = weight_grad(attended_cross_low, grad_cross_low)
@@ -326,17 +377,6 @@
         "qbhk,qbhd->kbhd", cross_probs_low, grad_attended_cross, preferred_element_type=jnp.float32
     ).reshape(frame_count, batch_count, D)
     grad_memory_kv = jnp.concatenate((grad_memory_keys, grad_memory_values), axis=2)
-    summed_kv = rounded(lax.psum(grad_memory_kv.astype(jnp.bfloat16), "seq").astype(jnp.float32))
-    memory_grad = (
-        project_back(summed_kv[:, :, :D].reshape(frame_count * batch_count, D), back_cross_key)
-        + project_back(summed_kv[:, :, D:].reshape(frame_count * batch_count, D), back_cross_value)
-    ).reshape(frame_count, batch_count, D)
-    part_kv = lax.dynamic_slice_in_dim(summed_kv, frame_start, frame_part, 0)
-    part_flat_keys = part_kv[:, :, :D].reshape(frame_part * batch_count, D)
-    part_flat_values = part_kv[:, :, D:].reshape(frame_part * batch_count, D)
-    grad_cross_key_weight = weight_grad(memory_part, part_flat_keys)
-    grad_cross_value_weight = weight_grad(memory_part, part_flat_values)
-    grad_cross_value_bias = column_sums(part_flat_values)
     grad_cross_query_weight = weight_grad(normed_cross_low, grad_cross_queries)
     grad_cross_query_bias = column_sums(grad_cross_queries)
     grad_normed_cross = project_back(grad_cross_queries, back_cross_query)
@@ -345,10 +385,10 @@
     )
     grad_middle = grad_after + grad_rows_cross
     back_query, back_key, back_value, back_self_out = (
-        lax.all_gather(query_weight, ("dp", "seq"), axis=0, tiled=True),
-        lax.all_gather(key_weight, ("dp", "seq"), axis=0, tiled=True),
-        lax.all_gather(value_weight, ("dp", "seq"), axis=0, tiled=True),
-        lax.all_gather(attn_out_weight, ("dp", "seq"), axis=0, tiled=True),
+        full_query,
+        full_key,
+        full_value,
+        full_self_out,
     )
     grad_self_low = rounded(grad_middle)
     grad_attn_out_weight = weight_grad(attended_self_low, grad_self_low)
@@ -370,8 +410,8 @@
     zero_query_grad = jnp.zeros((local_len, batch_count, HEADS, HEAD), jnp.float32)
     back_state = (zero_query_grad, jnp.zeros((full_length, batch_count, 2 * D), jnp.float32))
     running = back_state
-    self_key_piece = lax.all_gather(key_rows, "seq", axis=0, tiled=True)
-    self_value_piece = lax.all_gather(value_rows, "seq", axis=0, tiled=True)
+    self_key_piece = key_piece
+    self_value_piece = value_piece
     self_block_rows = math.gcd(self_key_piece.shape[0], 512)
 
     def back_block(inner_state, block_index):
@@ -405,11 +445,29 @@
         back_block, running, jnp.arange(self_key_piece.shape[0] // self_block_rows, dtype=jnp.int32)
     )
     grad_query_sum = running[0]
-    own_kv = lax.psum_scatter(
-        running[1].astype(jnp.bfloat16), "seq", scatter_dimension=0, tiled=True
-    ).astype(jnp.float32)
-    grad_key_low = rounded(own_kv[:, :, :D].reshape(token_count, D))
-    grad_value_low = rounded(own_kv[:, :, D:].reshape(token_count, D))
+    joint_kv = jnp.concatenate(
+        (
+            running[1].astype(jnp.bfloat16).reshape(seq_count, local_len, batch_count, 2 * D),
+            grad_memory_kv.astype(jnp.bfloat16).reshape(
+                seq_count, frame_part, batch_count, 2 * D
+            ),
+        ),
+        axis=1,
+    )
+    own_joint = lax.psum_scatter(joint_kv, "seq", scatter_dimension=0, tiled=False)
+    own_kv = own_joint[:local_len]
+    part_kv = own_joint[local_len:]
+    grad_key_low = own_kv[:, :, :D].reshape(token_count, D)
+    grad_value_low = own_kv[:, :, D:].reshape(token_count, D)
+    part_flat_keys = part_kv[:, :, :D].reshape(frame_part * batch_count, D)
+    part_flat_values = part_kv[:, :, D:].reshape(frame_part * batch_count, D)
+    part_memory_grad = (
+        project_back(part_flat_keys, back_cross_key)
+        + project_back(part_flat_values, back_cross_value)
+    ).reshape(frame_part, batch_count, D)
+    grad_cross_key_weight = weight_grad(memory_part, part_flat_keys)
+    grad_cross_value_weight = weight_grad(memory_part, part_flat_values)
+    grad_cross_value_bias = column_sums(part_flat_values)
     grad_query_low = rounded(grad_query_sum.reshape(token_count, D))
     grad_query_weight = weight_grad(normed_self_low, grad_query_low)
     grad_query_bias = column_sums(grad_query_low)
@@ -425,33 +483,93 @@
         grad_normed_self, scaled_self, inverse_self, full_self_gain.astype(jnp.float32)
     )
     token_grad = (grad_middle + grad_rows_self).reshape(local_len, batch_count, D)
-    owned_grads = (
-        lax.psum_scatter(grad_self_gain, ("dp", "seq"), scatter_dimension=0, tiled=True),
-        lax.psum_scatter(grad_self_shift, ("dp", "seq"), scatter_dimension=0, tiled=True),
-        lax.psum_scatter(grad_query_weight, ("dp", "seq"), scatter_dimension=0, tiled=True),
-        lax.psum_scatter(grad_query_bias, ("dp", "seq"), scatter_dimension=0, tiled=True),
-        lax.psum_scatter(grad_key_weight, ("dp", "seq"), scatter_dimension=0, tiled=True),
-        lax.psum_scatter(grad_value_weight, ("dp", "seq"), scatter_dimension=0, tiled=True),
-        lax.psum_scatter(grad_value_bias, ("dp", "seq"), scatter_dimension=0, tiled=True),
-        lax.psum_scatter(grad_attn_out_weight, ("dp", "seq"), scatter_dimension=0, tiled=True),
-        lax.psum_scatter(grad_attn_out_bias, ("dp", "seq"), scatter_dimension=0, tiled=True),
-        lax.psum_scatter(grad_cross_gain, ("dp", "seq"), scatter_dimension=0, tiled=True),
-        lax.psum_scatter(grad_cross_shift, ("dp", "seq"), scatter_dimension=0, tiled=True),
-        lax.psum_scatter(grad_cross_query_weight, ("dp", "seq"), scatter_dimension=0, tiled=True),
-        lax.psum_scatter(grad_cross_query_bias, ("dp", "seq"), scatter_dimension=0, tiled=True),
-        lax.psum_scatter(grad_cross_key_weight, ("dp", "seq"), scatter_dimension=0, tiled=True),
-        lax.psum_scatter(grad_cross_value_weight, ("dp", "seq"), scatter_dimension=0, tiled=True),
-        lax.psum_scatter(grad_cross_value_bias, ("dp", "seq"), scatter_dimension=0, tiled=True),
-        lax.psum_scatter(grad_cross_out_weight, ("dp", "seq"), scatter_dimension=0, tiled=True),
-        lax.psum_scatter(grad_cross_out_bias, ("dp", "seq"), scatter_dimension=0, tiled=True),
-        lax.psum_scatter(grad_mlp_gain, ("dp", "seq"), scatter_dimension=0, tiled=True),
-        lax.psum_scatter(grad_mlp_shift, ("dp", "seq"), scatter_dimension=0, tiled=True),
-        lax.psum_scatter(grad_fc_in_weight, ("dp", "seq"), scatter_dimension=0, tiled=True),
-        lax.psum_scatter(grad_fc_in_bias, ("dp", "seq"), scatter_dimension=0, tiled=True),
-        lax.psum_scatter(grad_fc_out_weight, ("dp", "seq"), scatter_dimension=0, tiled=True),
-        lax.psum_scatter(grad_fc_out_bias, ("dp", "seq"), scatter_dimension=0, tiled=True),
-    )
-    return (output, token_grad, memory_grad) + tuple(owned_grads)
+    def owner_rows(matrix):
+        return matrix.astype(jnp.bfloat16).reshape(owners, -1, D)
+
+    late_vectors = jnp.concatenate(
+        tuple(
+            vector.reshape(owners, -1)
+            for vector in (
+                grad_self_gain,
+                grad_self_shift,
+                grad_query_bias,
+                grad_value_bias,
+                grad_attn_out_bias,
+                grad_cross_gain,
+                grad_cross_shift,
+                grad_cross_query_bias,
+                grad_cross_value_bias,
+                grad_cross_out_bias,
+                grad_mlp_gain,
+                grad_mlp_shift,
+                grad_fc_out_bias,
+                grad_fc_in_bias,
+            )
+        ),
+        axis=1,
+    )
+    late_block = jnp.pad(
+        late_vectors.astype(jnp.bfloat16),
+        ((0, 0), (0, vector_rows * D - late_vectors.shape[1])),
+    ).reshape(owners, vector_rows, D)
+    late_grads = jnp.concatenate(
+        (
+            owner_rows(grad_query_weight),
+            owner_rows(grad_key_weight),
+            owner_rows(grad_value_weight),
+            owner_rows(grad_attn_out_weight),
+            owner_rows(grad_cross_query_weight),
+            owner_rows(grad_cross_key_weight),
+            owner_rows(grad_cross_value_weight),
+            owner_rows(grad_cross_out_weight),
+            late_block,
+        ),
+        axis=1,
+    )
+    owned_late = lax.psum_scatter(
+        late_grads, ("dp", "seq"), scatter_dimension=0, tiled=False
+    ).astype(jnp.float32)
+    memory_grad = lax.all_gather(
+        part_memory_grad.astype(jnp.bfloat16), "seq", axis=0, tiled=True
+    ).astype(jnp.float32)
+    owned_vectors = owned_late[8 * shard_rows :].reshape(-1)
+
+    def own_square(slot):
+        return owned_late[slot * shard_rows : (slot + 1) * shard_rows]
+
+    def own_vector(slot):
+        return owned_vectors[slot * shard_rows : (slot + 1) * shard_rows]
+
+    owned_fc_in_bias = owned_vectors[13 * shard_rows : 13 * shard_rows + fc_in_bias.shape[0]]
+    return (
+        output,
+        token_grad,
+        memory_grad,
+        own_vector(0),
+        own_vector(1),
+        own_square(0),
+        own_vector(2),
+        own_square(1),
+        own_square(2),
+        own_vector(3),
+        own_square(3),
+        own_vector(4),
+        own_vector(5),
+        own_vector(6),
+        own_square(4),
+        own_vector(7),
+        own_square(5),
+        own_square(6),
+        own_vector(8),
+        own_square(7),
+        own_vector(9),
+        own_vector(10),
+        own_vector(11),
+        owned_fc_in,
+        owned_fc_in_bias,
+        owned_fc_out,
+        own_vector(12),
+    )
 
 
 def solution(mesh):

time: 2210 us -> 1120 us (0.51)
  waiting for transfers between devices: 1700 us -> 583 us
  local copies, waits for them, and re-layouts: 101 us -> 217 us
  blocking collectives: 84.3 us -> 0 us
  matrix products: 232 us -> 203 us
    reduce_scatter x11 -> x3, waiting for transfers between devices: 1110 us -> 349 us  [the longest x1 127 us: local(): lax.psum_scatter(joint_kv, 'seq', scatter_dimension=0, tiled=False)]
    all_gather x12 -> x3, waiting for transfers between devices: 500 us -> 234 us  [the longest x1 126 us: local(): gathered = lax.all_gather(packed, ('dp', 'seq'), axis=0, tiled=False)]
    unnamed x2 -> x0, blocking collectives: 84.3 us -> none
    psum x1 -> x0, waiting for transfers between devices: 75.4 us -> none  [local(): lax.psum(grad_memory_kv.astype(jnp.bfloat16), 'seq').astype(jnp.float32)]
    reshape x0 -> x19, local copies, waits for them, and re-layouts: none -> 35.9 us  [the longest x1 22 us: local(): grad_fc_in_weight.astype(jnp.bfloat16)]
    concatenate x0 -> x7, local copies, waits for them, and re-layouts: none -> 31 us  [the longest x3 20.7 us: local(): jnp.concatenate((grad_memory_keys, grad_memory_values), axis=2)]
    slice x0 -> x12, local copies, waits for them, and re-layouts: none -> 26.3 us  [the longest x1 7.02 us: square_at(): gathered[:, slot * shard_rows:(slot + 1) * shard_rows, :].reshape(D, D)]
    unnamed x222 -> x277, local copies, waits for them, and re-layouts: 69.1 us -> 70.8 us
  transfers between devices with their start and end apart: 24 -> 6, of which waited for: 21 -> 6; matrix products, arithmetic and copies ran while one was open for 14% -> 14% of each run, Pallas kernels for 0% -> 0%
where the time goes in v1:
time: 1120 us; the launch traced here: 1110 us
  waiting for transfers between devices  583 us (52%)
  local copies, waits for them, and re-layouts  217 us (19%)
  matrix products  203 us (18%)
  other arithmetic  83.7 us (7%)
  between operations  16.6 us (1%)
    reduce_scatter x1, waiting for transfers between devices, local(): lax.psum_scatter(joint_kv, 'seq', scatter_dimension=0, tiled=False)  127 us
    all_gather x1, waiting for transfers between devices, local(): gathered = lax.all_gather(packed, ('dp', 'seq'), axis=0, tiled=False)  126 us
    reduce_scatter x1, waiting for transfers between devices, local(): lax.psum_scatter(late_grads, ('dp', 'seq'), scatter_dimension=0, tiled=Fa...  114 us
    reduce_scatter x1, waiting for transfers between devices, local(): lax.psum_scatter(early_grads, ('dp', 'seq'), scatter_dimension=0, tiled=F...  108 us
    unnamed x277, local copies, waits for them, and re-layouts  70.8 us
    all_gather x1, waiting for transfers between devices, local(): lax.all_gather(jnp.concatenate((key_rows, value_rows), axis=2), 'seq', ax...  61.5 us
    all_gather x1, waiting for transfers between devices, local(): lax.all_gather(part_memory_grad.astype(jnp.bfloat16), 'seq', axis=0, tile...  46.7 us
    dot_general x10, matrix products, project(): return jnp.dot(left_rows, matrix, preferred_element_type=jnp.float32)  32.6 us
  transfers between devices with their start and end apart: 6, of which 6 were waited for; matrix products, arithmetic and copies ran while one was open for 14% of the time, Pallas kernels for 0%

profile of v1, /device:TPU:0, one launch (start us, length us, event | category | flops | bytes accessed | tf_op | source)
XLA Modules:
  0.0 1110.2 jit_solution(16645139889997488787)
XLA Ops:
  9.1 9.4 concatenate.42
  28.3 126.1 %all-gather.8.cloned.1.call-done = bf16[12544,768]{1,0:T(8,128)(2,1)} async-done(((bf16[392,768]{1,0:T(8,128)(2,1)}), bf16[12544,768]{1,0:T(8,128)(2,1)}) %all-gather.8.cloned.1.call-update) | async-done | bytes 19267600 | tf_op jit(solution)/shard_map/all_gather | solution.py:155
  155.4 7.0 fusion.146
  183.2 6.6 fusion.145
  192.2 3.3 copy.165
  196.8 4.9 convolution_convert_fusion.2
  201.7 3.6 add_convert_fusion
  205.3 61.5 %all-gather.6.cloned.1.call-done = bf16[2048,1,1536]{2,0,1:T(8,128)(2,1)} async-done(((bf16[256,1,1536]{2,0,1:T(8,128)(2,1)}), bf16[2048,1,1536]{2,0,1:T(8,128)(2,1)}) %all-gather.6.cloned.1.call-update) | async-done | bytes 6291472 | tf_op jit(solution)/shard_map/all_gather | solution.py:221
  266.7 6.0 fusion.147
  272.7 4.9 copy.134
  277.6 4.8 copy.135
  282.3 63.7 %while.28 = (s32[]{:T(128)}, f32[256,1,12]{0,2,1:T(8,128)S(1)}, f32[256,1,12]{0,2,1:T(8,128)S(1)}, f32[256,1,12,64]{0,3,2,1:T(8,128)}, s32[4]{0:T(128)S(1)}, /*i...) while((s32[]{:T(128)}, f32[256,1,12]{0,2,1:T(8,128)S(1)}, ...), condition=%wide.region_7.8_spmd.clone, body=%wide.region_3.7_spmd.clone.sunk | while | flops 421095424 | bytes 51460936 | solution.py:246
  286.3 3.8 fusion.230
  290.1 4.2 fusion.232
  294.7 3.4 fusion.233
  302.0 3.8 fusion.230
  305.9 4.2 fusion.232
  310.4 3.6 fusion.233
  318.0 3.8 fusion.230
  321.8 4.2 fusion.232
  326.4 3.6 fusion.233
  334.0 3.8 fusion.230
  337.8 4.2 fusion.232
  342.4 3.6 fusion.233
  354.4 6.0 fusion.53
  360.4 5.1 fusion.57
  367.2 7.5 fusion.86
  375.8 9.5 multiply_convert_fusion
  385.3 5.0 fusion.151
  395.9 15.5 %fusion.49 = (f32[256,12]{0,1:T(8,128)S(1)}, f32[12,1536,256]{2,1,0:T(8,128)}) fusion(f32[256,12]{0,1:T(8,128)S(1)} %copy-done.72, f32[256,12]{0,1:T(8,128)S(1)} %get-tuple-element.576, f32[12,1536,256]{2,1,0:T(8,128)} %copy-done.3, pred[1536]{0:T(1024)(128)(4,1)S(1)} %copy-done.83, bf16[1536,12,64]{0,2,1:T(8,128)(2,1)} %bitcast.608, ...), kind=kOutput, calls=%fused_computation.72 | convolution fusion | flops 632288256 | bytes 40539648 | tf_op jit(solution)/shard_map/qbhd,kbhd->qbhk/dot_general | solution.py:357
  411.4 10.4 fusion.74
  421.9 10.8 fusion.58
  432.7 3.7 copy-done.5
  438.8 8.3 fusion.73
  454.0 3.4 broadcast_in_dim.90
  457.5 74.1 %while.29 = (s32[]{:T(128)}, f32[256,1,12,64]{0,3,2,1:T(8,128)}, bf16[2048,1,1536]{0,2,1:T(8,128)(2,1)}, s32[4]{0:T(128)S(1)}, bf16[2048,1,768]{0,2,1:T(8,128)(2...) while((s32[]{:T(128)}, f32[256,1,12,64]{0,3,2,1:T(8,128)}, ...), condition=%wide.region_22.23_spmd.clone, body=%wide.region_20.22_spmd.clone.sunk | while | flops 1028005888 | bytes 84216896 | solution.py:444
  462.0 3.9 fusion.246
  465.9 3.5 fusion.247
  469.4 4.3 fusion.248
  480.3 3.9 fusion.246
  484.2 3.7 fusion.247
  487.9 4.3 fusion.248
  498.8 3.9 fusion.246
  502.7 3.7 fusion.247
  506.4 4.3 fusion.248
  517.3 3.9 fusion.246
  521.2 3.7 fusion.247
  524.9 4.3 fusion.248
  531.6 5.9 concatenate.46
  537.5 6.0 concatenate.45
  543.5 8.2 pad_maximum_fusion.2
  551.7 8.7 copy.147
  560.5 8.7 copy.144
  569.1 9.6 pad_maximum_fusion
  579.8 5.5 convolution_convert_fusion.1
  585.4 22.0 %reshape.1439 = bf16[32,24,4,768]{3,2,1,0:T(4,128)(2,1)} reshape(bf16[768,3072]{1,0:T(8,128)(2,1)} %convolution_convert_fusion.1) | data formatting | bytes 9437184 | tf_op jit(solution)/shard_map/reshape | solution.py:327
  607.4 3.4 copy.148
  612.3 4.0 pad_maximum_fusion.1
  636.1 126.6 %reduce-scatter.4.cloned.1.call-done = bf16[1,448,1,1536]{3,1,2,0:T(8,128)(2,1)} async-done(((bf16[8,448,1,1536]{3,1,2,0:T(8,128)(2,1)}), bf16[1,448,1,1536]{3,1,2,0:T(8,128)(2,1)}) %reduce-scatter.4.cloned.1.call-update) | async-done | bytes 1376272 | tf_op jit(solution)/shard_map/reduce_scatter | solution.py:457
  790.7 5.3 fusion.92
  796.0 108.0 %reduce-scatter.8.cloned.1.call-done = bf16[1,192,768]{2,1,0:T(8,128)(2,1)} async-done(((bf16[32,192,768]{2,1,0:T(8,128)(2,1)}), bf16[1,192,768]{2,1,0:T(8,128)(2,1)}) %reduce-scatter.8.cloned.1.call-update) | async-done | bytes 294928 | tf_op jit(solution)/shard_map/reduce_scatter | solution.py:336
  910.2 46.7 %all-gather.10.cloned.1.call-done = bf16[1536,768]{1,0:T(8,128)(2,1)} async-done(((bf16[192,768]{1,0:T(8,128)(2,1)}), bf16[1536,768]{1,0:T(8,128)(2,1)}) %all-gather.10.cloned.1.call-update) | async-done | bytes 2359312 | tf_op jit(solution)/shard_map/all_gather | solution.py:532
  958.9 26.4 %copy.151 = f32[1536,1,768]{2,1,0:T(1,128)} copy(f32[1536,1,768]{2,0,1:T(8,128)S(1)} %bitcast_convert_fusion) | data formatting | bytes 9437184
  985.3 114.1 %reduce-scatter.6.cloned.1.call-done = bf16[1,200,768]{2,1,0:T(8,128)(2,1)} async-done(((bf16[32,200,768]{2,1,0:T(8,128)(2,1)}), bf16[1,200,768]{2,1,0:T(8,128)(2,1)}) %reduce-scatter.6.cloned.1.call-update) | async-done | bytes 307216 | tf_op jit(solution)/shard_map/reduce_scatter | solution.py:529
  (572 shorter events, 161.4 us)
Async XLA Ops:
  7.2 189.6 %copy-start = (bf16[1536,1,768]{2,0,1:T(8,128)(2,1)S(1)}, bf16[1536,1,768]{2,0,1:T(8,128)(2,1)}, u32[]{:S(2)}) copy-start(bf16[1536,1,768]{2,0,1:T(8,128)(2,1)} %param.34) | copy-start | bytes 7077892
  7.2 147.2 %all-gather.8.cloned.1.call-start = ((), (), s32[]{:S(2)}) async-start(), calls=%async_computation.7 | async-start | bytes 19869696 | tf_op jit(solution)/shard_map/all_gather | solution.py:155
  25.8 240.9 %all-gather.6.cloned.1.call-start = ((), (), s32[]{:S(2)}) async-start(), calls=%async_computation.3 | async-start | bytes 7077888 | tf_op jit(solution)/shard_map/all_gather | solution.py:221
  27.0 139.7 %copy-start.115 = (f32[256]{0:T(256)}, f32[256]{0:T(256)S(1)}, u32[]{:S(2)}) copy-start(f32[256]{0:T(256)S(1)} %broadcast_multiply_fusion.8) | copy-start | bytes 3076
  28.3 138.5 %copy-start.121 = (f32[256]{0:T(256)}, f32[256]{0:T(256)S(1)}, u32[]{:S(2)}) copy-start(f32[256]{0:T(256)S(1)} %add_rsqrt_fusion.2) | copy-start | bytes 3076
  155.4 9.5 copy-start.26
  164.8 4.8 copy-start.125
  164.9 4.7 copy-start.102
  169.6 593.0 %reduce-scatter.4.cloned.1.call-start = ((), (), s32[]{:S(2)}) async-start(), calls=%async_computation.4 | async-start | bytes 12386304 | tf_op jit(solution)/shard_map/reduce_scatter | solution.py:457
  171.9 7.6 copy-start.79
  171.9 7.7 copy-start.78
  171.9 8.4 copy-start.77
  171.9 9.1 copy-start.76
  196.8 4.9 copy-start.33
  277.6 4.8 copy-start.58
  277.6 4.8 copy-start.80
  290.1 4.6 copy-start.1
  346.0 6.4 copy-start.6
  346.0 6.4 copy-start.47
  346.1 5.0 copy-start.56
  346.1 5.0 copy-start.84
  346.1 5.0 copy-start.107
  346.1 5.0 copy-start.127
  350.2 24.6 %copy-start.10 = (f32[256,768]{1,0:T(8,128)}, f32[256,768]{1,0:T(8,128)S(1)}, u32[]{:S(2)}) copy-start(f32[256,768]{1,0:T(8,128)S(1)} %get-tuple-element.575) | copy-start | bytes 2359300
  354.4 6.0 copy-start.82
  360.4 6.8 copy-start.3
  365.6 10.1 slice-start.5
  367.2 7.6 copy-start.23
  367.2 7.6 copy-start.109
  367.2 8.5 slice-start.6
  374.8 10.5 copy-start.51
  375.4 17.1 %copy-start.13 = (f32[256,768]{1,0:T(8,128)}, f32[256,768]{1,0:T(8,128)S(1)}, u32[]{:S(2)}) copy-start(f32[256,768]{1,0:T(8,128)S(1)} %get-tuple-element.579) | copy-start | bytes 2359300
  375.4 17.1 %copy-start.96 = (f32[256]{0:T(256)}, f32[256]{0:T(256)S(1)}, u32[]{:S(2)}) copy-start(f32[256]{0:T(256)S(1)} %broadcast_multiply_fusion.6) | copy-start | bytes 3076
  375.7 16.9 %copy-start.112 = (f32[256]{0:T(256)}, f32[256]{0:T(256)S(1)}, u32[]{:S(2)}) copy-start(f32[256]{0:T(256)S(1)} %add_rsqrt_fusion) | copy-start | bytes 3076
  375.7 9.5 copy-start.61
  395.9 26.0 %slice-start = ((s8[18874368]{0:T(1024)(128)(4,1)}), s8[4194304]{0:T(1024)(128)(4,1)S(1)}, s32[]{:S(2)}) async-start(s8[18874368]{0:T(1024)(128)(4,1)} %bitcast.517), calls=%async_computation.9 | async-start | bytes 8388608
  395.9 26.0 %slice-start.1 = ((s8[18874368]{0:T(1024)(128)(4,1)}), s8[4194304]{0:T(1024)(128)(4,1)S(1)}, s32[]{:S(2)}) async-start(s8[18874368]{0:T(1024)(128)(4,1)} %bitcast.517), calls=%async_computation.10 | async-start | bytes 8388608
  395.9 26.0 %slice-start.2 = ((s8[18874368]{0:T(1024)(128)(4,1)}), s8[2097152]{0:T(1024)(128)(4,1)S(1)}, s32[]{:S(2)}) async-start(s8[18874368]{0:T(1024)(128)(4,1)} %bitcast.517), calls=%async_computation.11 | async-start | bytes 4194304
  411.4 10.5 slice-start.3
  411.4 10.5 slice-start.4
  421.9 14.5 %copy-start.9 = (bf16[768,1536]{1,0:T(8,128)(2,1)S(1)}, bf16[768,1536]{1,0:T(8,128)(2,1)}, u32[]{:S(2)}) copy-start(bf16[768,1536]{1,0:T(8,128)(2,1)} %convolution_convert_fusion.2) | copy-start | bytes 7077892
  438.7 8.3 copy-start.46
  438.7 8.3 copy-start.11
  438.7 8.3 copy-start.57
  438.7 8.3 copy-start.85
  438.7 8.3 copy-start.100
  438.7 8.3 copy-start.120
  578.8 325.2 %reduce-scatter.8.cloned.1.call-start = ((), (), s32[]{:S(2)}) async-start(), calls=%async_computation.6 | async-start | bytes 9732096 | tf_op jit(solution)/shard_map/reduce_scatter | solution.py:336
  616.3 6.1 copy-start.108
  616.3 13.7 %copy-start.27 = (bf16[256,1,768]{2,0,1:T(8,128)(2,1)S(1)}, bf16[256,1,768]{2,0,1:T(8,128)(2,1)}, u32[]{:S(2)}) copy-start(bf16[256,1,768]{2,0,1:T(8,128)(2,1)} %param.33) | copy-start | bytes 1179652
  616.3 13.7 %copy-start.103 = (f32[768]{0:T(1024)S(1)}, f32[768]{0:T(1024)}, u32[]{:S(2)}) copy-start(f32[768]{0:T(1024)} %copy-done.102) | copy-start | bytes 9220
  616.3 340.5 %all-gather.10.cloned.1.call-start = ((), (), s32[]{:S(2)}) async-start(), calls=%async_computation.8 | async-start | bytes 2654208 | tf_op jit(solution)/shard_map/all_gather | solution.py:532
  618.2 14.8 %copy-start.17 = (f32[256,768]{1,0:T(8,128)S(1)}, f32[256,768]{1,0:T(8,128)}, u32[]{:S(2)}) copy-start(f32[256,768]{1,0:T(8,128)} %copy-done.16) | copy-start | bytes 2359300
  763.8 5.5 copy-start.12
  763.8 5.5 copy-start.86
  763.8 5.5 copy-start.101
  767.2 332.2 %reduce-scatter.6.cloned.1.call-start = ((), (), s32[]{:S(2)}) async-start(), calls=%async_computation.5 | async-start | bytes 10137600 | tf_op jit(solution)/shard_map/reduce_scatter | solution.py:529
  767.3 4.9 copy-start.54
  767.3 5.0 copy-start.32
  790.7 117.4 %copy-start.128 = (f32[256]{0:T(256)S(1)}, f32[256]{0:T(256)}, u32[]{:S(2)}) copy-start(f32[256]{0:T(256)} %get-tuple-element.453) | copy-start | bytes 3076
  790.7 117.4 %copy-start.106 = (f32[768]{0:T(1024)S(1)}, f32[768]{0:T(1024)}, u32[]{:S(2)}) copy-start(f32[768]{0:T(1024)} %copy-done.102) | copy-start | bytes 9220
  790.7 117.4 %copy-start.118 = (f32[256]{0:T(256)S(1)}, f32[256]{0:T(256)}, u32[]{:S(2)}) copy-start(f32[256]{0:T(256)} %copy-done.115) | copy-start | bytes 3076
  790.7 117.4 %copy-start.124 = (f32[256]{0:T(256)S(1)}, f32[256]{0:T(256)}, u32[]{:S(2)}) copy-start(f32[256]{0:T(256)} %copy-done.121) | copy-start | bytes 3076
  796.0 112.2 %copy-start.18 = (f32[256,768]{1,0:T(8,128)S(1)}, f32[256,768]{1,0:T(8,128)}, u32[]{:S(2)}) copy-start(f32[256,768]{1,0:T(8,128)} %copy-done.16) | copy-start | bytes 2359300
  (108 other events, 308.7 us)
Sparse Core Ops, SparseCore 0:
  25.9 128.3 all-gather.7
  169.7 96.9 all-gather.5
  578.9 183.6 reduce-scatter.3
  768.4 135.5 reduce-scatter.7
  906.0 50.7 all-gather.9
  962.6 136.7 reduce-scatter.5

commit v2 on v1

--- a/solution.py
+++ b/solution.py
@@ -3,6 +3,8 @@
 import jax
 import jax.numpy as jnp
 from jax import lax
+from jax.experimental import pallas as pl
+from jax.experimental.pallas import tpu as pltpu
 from jax.sharding import PartitionSpec as P
 
 D = 768
@@ -71,6 +73,638 @@
     query_side = jnp.transpose(query_label)[:, :, None]
     same_piece = (query_side == key_label[None, :, :]) & (query_side > 0)
     return (causal | same_piece)[:, :, None, :]
+
+
+PAIR = 2 * HEAD
+QUERY_BLOCK = 256
+
+
+def to_pairs(rows, seq_count):
+    blocks = jnp.transpose(rows.reshape(rows.shape[0], D // PAIR, PAIR), (1, 0, 2))
+    return jnp.pad(blocks, ((0, seq_count - D // PAIR), (0, 0), (0, 0)))
+
+
+def from_pairs(blocks):
+    kept = blocks[: D // PAIR]
+    return jnp.transpose(kept, (1, 0, 2)).reshape(kept.shape[1], D)
+
+
+def dot_rows(left, right):
+    return lax.dot_general(left, right, (((1,), (1,)), ((), ())), preferred_element_type=jnp.float32)
+
+
+def dot_plain(left, right):
+    return lax.dot_general(left, right, (((1,), (0,)), ((), ())), preferred_element_type=jnp.float32)
+
+
+def dot_columns(left, right):
+    return lax.dot_general(left, right, (((0,), (0,)), ((), ())), preferred_element_type=jnp.float32)
+
+
+def split_pair(block):
+    lanes = lax.broadcasted_iota(jnp.int32, block.shape, 1)
+    zero = jnp.zeros_like(block)
+    return (jnp.where(lanes < HEAD, block, zero), jnp.where(lanes < HEAD, zero, block))
+
+
+def join_pair(first, second, shape):
+    lanes = lax.broadcasted_iota(jnp.int32, shape, 1)
+    return jnp.where(lanes < HEAD, first, second)
+
+
+def block_allowed(query_block, key_block, query_label, key_label):
+    shape = (QUERY_BLOCK, QUERY_BLOCK)
+    query_pos = query_block * QUERY_BLOCK + lax.broadcasted_iota(jnp.int32, shape, 0)
+    key_pos = key_block * QUERY_BLOCK + lax.broadcasted_iota(jnp.int32, shape, 1)
+    same_piece = (query_label == key_label) & (query_label > 0)
+    return (key_pos <= query_pos) | same_piece
+
+
+def self_forward_body(query_ref, key_ref, value_ref, column_ref, row_ref, out_ref, log_ref):
+    block = pl.program_id(0)
+    block_count = pl.num_programs(0)
+    query_halves = split_pair(query_ref[...])
+    query_label = column_ref[...]
+
+    def step(key_block, state, masked):
+        start = pl.multiple_of(key_block * QUERY_BLOCK, QUERY_BLOCK)
+        keys = key_ref[pl.ds(start, QUERY_BLOCK), :]
+        value_halves = split_pair(value_ref[pl.ds(start, QUERY_BLOCK), :])
+        maxima, totals, weighted = state
+        new_maxima, new_totals, factors, added = [], [], [], []
+        if masked:
+            allowed = block_allowed(
+                block, key_block, query_label, row_ref[:, pl.ds(start, QUERY_BLOCK)]
+            )
+        for half in range(2):
+            scores = dot_rows(query_halves[half], keys) * 0.125
+            if masked:
+                scores = jnp.where(allowed, scores, neg_large)
+            new_max = jnp.maximum(maxima[half], jnp.max(scores, axis=1, keepdims=True))
+            exp_terms = jnp.exp(scores - new_max)
+            factor = jnp.exp(maxima[half] - new_max)
+            new_maxima.append(new_max)
+            new_totals.append(totals[half] * factor + jnp.sum(exp_terms, axis=1, keepdims=True))
+            factors.append(factor)
+            added.append(dot_plain(rounded(exp_terms), value_halves[half]))
+        weighted = weighted * join_pair(factors[0], factors[1], weighted.shape)
+        return (tuple(new_maxima), tuple(new_totals), weighted + added[0] + added[1])
+
+    column = (QUERY_BLOCK, 1)
+    state = (
+        (jnp.full(column, neg_large, jnp.float32),) * 2,
+        (jnp.zeros(column, jnp.float32),) * 2,
+        jnp.zeros((QUERY_BLOCK, PAIR), jnp.float32),
+    )
+    state = lax.fori_loop(0, block, lambda index, state: step(index, state, False), state)
+    last = jnp.minimum(block + 2, block_count)
+    state = lax.fori_loop(block, last, lambda index, state: step(index, state, True), state)
+    maxima, totals, weighted = state
+    out_ref[...] = weighted / join_pair(totals[0], totals[1], weighted.shape)
+    log_ref[...] = join_pair(
+        maxima[0] + jnp.log(totals[0]), maxima[1] + jnp.log(totals[1]), weighted.shape
+    )
+
+
+def self_forward(queries, keys, values, labels):
+    length = queries.shape[0]
+    block_spec = pl.BlockSpec((QUERY_BLOCK, PAIR), lambda index: (index, 0))
+    whole_spec = pl.BlockSpec((length, PAIR), lambda index: (0, 0))
+    result = jax.ShapeDtypeStruct((length, PAIR), jnp.float32)
+    return pl.pallas_call(
+        self_forward_body,
+        grid=(length // QUERY_BLOCK,),
+        in_specs=[
+            block_spec,
+            whole_spec,
+            whole_spec,
+            pl.BlockSpec((QUERY_BLOCK, 1), lambda index: (index, 0)),
+            pl.BlockSpec((1, length), lambda index: (0, 0)),
+        ],
+        out_specs=[block_spec, block_spec],
+        out_shape=[result, result],
+        name="self_forward",
+    )(queries, keys, values, labels[:, None], labels[None, :])
+
+
+def self_backward_body(
+    query_ref,
+    key_ref,
+    value_ref,
+    column_ref,
+    row_ref,
+    out_ref,
+    log_ref,
+    grad_ref,
+    grad_query_ref,
+    grad_key_ref,
+    grad_value_ref,
+    key_sum,
+    value_sum,
+):
+    block = pl.program_id(0)
+    block_count = pl.num_programs(0)
+
+    @pl.when(block == 0)
+    def clear():
+        key_sum[...] = jnp.zeros_like(key_sum)
+        value_sum[...] = jnp.zeros_like(value_sum)
+
+    query_halves = split_pair(query_ref[...])
+    grad_rows = grad_ref[...]
+    grad_halves = split_pair(grad_rows)
+    query_label = column_ref[...]
+    products = grad_rows.astype(jnp.float32) * out_ref[...]
+    deltas = tuple(jnp.sum(part, axis=1, keepdims=True) for part in split_pair(products))
+    logs = (log_ref[:, :1], log_ref[:, HEAD : HEAD + 1])
+
+    def step(key_block, query_sum, masked):
+        start = pl.multiple_of(key_block * QUERY_BLOCK, QUERY_BLOCK)
+        here = pl.ds(start, QUERY_BLOCK)
+        keys = key_ref[here, :]
+        values = value_ref[here, :]
+        key_halves = split_pair(keys)
+        if masked:
+            allowed = block_allowed(block, key_block, query_label, row_ref[:, here])
+        key_add = jnp.zeros((QUERY_BLOCK, PAIR), jnp.float32)
+        value_add = jnp.zeros((QUERY_BLOCK, PAIR), jnp.float32)
+        for half in range(2):
+            scores = dot_rows(query_halves[half], keys) * 0.125
+            if masked:
+                scores = jnp.where(allowed, scores, neg_large)
+            probs = jnp.exp(scores - logs[half])
+            grad_probs = dot_rows(grad_halves[half], values)
+            grad_scores = rounded(probs * (grad_probs - deltas[half]) * 0.125)
+            query_sum = query_sum + dot_plain(grad_scores, key_halves[half])
+            key_add = key_add + dot_columns(grad_scores, query_halves[half])
+            value_add = value_add + dot_columns(rounded(probs), grad_halves[half])
+        key_sum[here, :] = key_sum[here, :] + key_add
+        value_sum[here, :] = value_sum[here, :] + value_add
+        return query_sum
+
+    query_sum = jnp.zeros((QUERY_BLOCK, PAIR), jnp.float32)
+    query_sum = lax.fori_loop(0, block, lambda index, total: step(index, total, False), query_sum)
+    last = jnp.minimum(block + 2, block_count)
+    query_sum = lax.fori_loop(block, last, lambda index, total: step(index, total, True), query_sum)
+    grad_query_ref[...] = rounded(query_sum)
+
+    @pl.when(block == block_count - 1)
+    def finish():
+        grad_key_ref[...] = rounded(key_sum[...])
+        grad_value_ref[...] = rounded(value_sum[...])
+
+
+def self_backward(queries, keys, values, labels, attended, log_total, grad_attended):
+    length = queries.shape[0]
+    block_spec = pl.BlockSpec((QUERY_BLOCK, PAIR), lambda index: (index, 0))
+    whole_spec = pl.BlockSpec((length, PAIR), lambda index: (0, 0))
+    result = jax.ShapeDtypeStruct((length, PAIR), jnp.bfloat16)
+    return pl.pallas_call(
+        self_backward_body,
+        grid=(length // QUERY_BLOCK,),
+        in_specs=[
+            block_spec,
+            whole_spec,
+            whole_spec,
+            pl.BlockSpec((QUERY_BLOCK, 1), lambda index: (index, 0)),
+            pl.BlockSpec((1, length), lambda index: (0, 0)),
+            block_spec,
+            block_spec,
+            block_spec,
+        ],
+        out_specs=[block_spec, whole_spec, whole_spec],
+        out_shape=[result, result, result],
+        scratch_shapes=[
+            pltpu.VMEM((length, PAIR), jnp.float32),
+            pltpu.VMEM((length, PAIR), jnp.float32),
+        ],
+        name="self_backward",
+    )(queries, keys, values, labels[:, None], labels[None, :], attended, log_total, grad_attended)
+
+
+def local_heads(
+    tokens,
+    memory,
+    piece_starts,
+    memory_lengths,
+    self_gain,
+    self_shift,
+    query_weight,
+    query_bias,
+    key_weight,
+    value_weight,
+    value_bias,
+    attn_out_weight,
+    attn_out_bias,
+    cross_gain,
+    cross_shift,
+    cross_query_weight,
+    cross_query_bias,
+    cross_key_weight,
+    cross_value_weight,
+    cross_value_bias,
+    cross_out_weight,
+    cross_out_bias,
+    mlp_gain,
+    mlp_shift,
+    fc_in_weight,
+    fc_in_bias,
+    fc_out_weight,
+    fc_out_bias,
+    out_grad,
+):
+    local_len, batch_count, model_width = tokens.shape
+    seq_count = lax.axis_size("seq")
+    seq_index = lax.axis_index("seq")
+    full_length = local_len * seq_count
+    token_count = local_len * batch_count
+    query_pos = seq_index * local_len + jnp.arange(local_len, dtype=jnp.int32)
+    labels = piece_labels(jnp.arange(full_length, dtype=jnp.int32), piece_starts).reshape(-1)
+    input_rows = tokens.reshape(token_count, D).astype(jnp.float32)
+    shard_rows = query_weight.shape[0]
+    wide_parts = fc_in_weight.shape[1] // D
+    vectors = jnp.concatenate(
+        (
+            self_gain,
+            self_shift,
+            query_bias,
+            value_bias,
+            attn_out_bias,
+            cross_gain,
+            cross_shift,
+            cross_query_bias,
+            cross_value_bias,
+            cross_out_bias,
+            mlp_gain,
+            mlp_shift,
+            fc_out_bias,
+            fc_in_bias,
+        )
+    )
+    vector_rows = 8
+    vector_block = jnp.pad(vectors, (0, vector_rows * D - vectors.shape[0])).reshape(vector_rows, D)
+    fc_in_blocks = jnp.transpose(
+        fc_in_weight.reshape(shard_rows, wide_parts, D), (1, 0, 2)
+    ).reshape(wide_parts * shard_rows, D)
+    first_packed = jnp.concatenate((query_weight, key_weight, value_weight, vector_block))
+    first = lax.all_gather(first_packed, ("dp", "seq"), axis=0, tiled=False)
+    owners = first.shape[0]
+
+    def first_at(slot):
+        return first[:, slot * shard_rows : (slot + 1) * shard_rows, :].reshape(D, D)
+
+    full_query, full_key, full_value = (first_at(slot) for slot in range(3))
+    full_vectors = first[:, 3 * shard_rows :, :].reshape(owners, vector_rows * D)
+    packed = jnp.concatenate(
+        (
+            attn_out_weight,
+            cross_query_weight,
+            cross_key_weight,
+            cross_value_weight,
+            cross_out_weight,
+            fc_in_blocks,
+            fc_out_weight,
+        )
+    )
+    packed, first = lax.optimization_barrier((packed, first))
+    gathered = lax.all_gather(packed, ("dp", "seq"), axis=0, tiled=False)
+
+    def square_at(slot):
+        return gathered[:, slot * shard_rows : (slot + 1) * shard_rows, :].reshape(D, D)
+
+    full_self_out, full_cross_query, full_cross_key, full_cross_value, full_cross_out = (
+        square_at(slot) for slot in range(5)
+    )
+    wide_start = 5 * shard_rows
+    wide_stop = wide_start + wide_parts * shard_rows
+    full_fc_in = jnp.transpose(
+        gathered[:, wide_start:wide_stop, :].reshape(owners, wide_parts, shard_rows, D),
+        (0, 2, 1, 3),
+    ).reshape(D, wide_parts * D)
+    out_stop = wide_stop + fc_out_weight.shape[0]
+    full_fc_out = gathered[:, wide_stop:out_stop, :].reshape(wide_parts * D, D)
+
+    def vector_at(slot):
+        return full_vectors[:, slot * shard_rows : (slot + 1) * shard_rows].reshape(D)
+
+    (
+        full_self_gain,
+        full_self_shift,
+        full_query_bias,
+        full_value_bias,
+        full_self_out_bias,
+        full_cross_gain,
+        full_cross_shift,
+        full_cross_query_bias,
+        full_cross_value_bias,
+        full_cross_out_bias,
+        full_mlp_gain,
+        full_mlp_shift,
+        full_fc_out_bias,
+    ) = (vector_at(slot) for slot in range(13))
+    full_fc_in_bias = full_vectors[
+        :, 13 * shard_rows : 13 * shard_rows + fc_in_bias.shape[0]
+    ].reshape(-1)
+    normed_self, scaled_self, inverse_self = norm_forward(
+        input_rows, full_self_gain.astype(jnp.float32), full_self_shift.astype(jnp.float32)
+    )
+    normed_self_low = rounded(normed_self)
+    query_rows = rounded(project(normed_self_low, full_query) + full_query_bias.astype(jnp.float32))
+    key_rows = rounded(project(normed_self_low, full_key))
+    value_rows = rounded(
+        project(normed_self_low, full_value) + full_value_bias.astype(jnp.float32)
+    )
+    head_triple = lax.all_to_all(
+        jnp.stack(
+            tuple(to_pairs(rows, seq_count) for rows in (query_rows, key_rows, value_rows)), axis=1
+        ),
+        "seq",
+        0,
+        0,
+    )
+    head_queries, head_keys, head_values = (
+        head_triple[:, slot].reshape(full_length, PAIR) for slot in range(3)
+    )
+    head_attended, head_log = self_forward(head_queries, head_keys, head_values, labels)
+    attended_blocks = lax.all_to_all(
+        rounded(head_attended).reshape(seq_count, local_len, PAIR), "seq", 0, 0
+    )
+    attended_self_low = from_pairs(attended_blocks)
+    middle_rows = (
+        input_rows
+        + project(attended_self_low, full_self_out)
+        + full_self_out_bias.astype(jnp.float32)
+    )
+    normed_cross, scaled_cross, inverse_cross = norm_forward(
+        middle_rows, full_cross_gain.astype(jnp.float32), full_cross_shift.astype(jnp.float32)
+    )
+    normed_cross_low = rounded(normed_cross)
+    cross_queries = rounded(
+        project(normed_cross_low, full_cross_query) + full_cross_query_bias.astype(jnp.float32)
+    ).reshape(local_len, batch_count, HEADS, HEAD)
+    frame_count = memory.shape[0]
+    frame_part = frame_count // seq_count
+    frame_start = seq_index * frame_part
+    memory_part = lax.dynamic_slice_in_dim(memory, frame_start, frame_part, 0).reshape(
+        frame_part * batch_count, D
+    )
+    memory_flat = memory.reshape(frame_count * batch_count, D)
+    memory_keys = rounded(project(memory_flat, full_cross_key)).reshape(frame_count, batch_count, D)
+    memory_values = rounded(
+        project(memory_flat, full_cross_value) + full_cross_value_bias.astype(jnp.float32)
+    ).reshape(frame_count, batch_count, D)
+    memory_key_heads = memory_keys.reshape(frame_count, batch_count, HEADS, HEAD)
+    memory_value_heads = memory_values.reshape(frame_count, batch_count, HEADS, HEAD)
+    frame_valid = (jnp.arange(frame_count, dtype=jnp.int32)[None, :] < memory_lengths[:, None])[
+        None, :, None, :
+    ]
+    cross_scores = (
+        jnp.einsum(
+            "qbhd,kbhd->qbhk", cross_queries, memory_key_heads, preferred_element_type=jnp.float32
+        )
+        * 0.125
+    )
+    cross_max = jnp.max(jnp.where(frame_valid, cross_scores, neg_large), axis=-1, keepdims=True)
+    cross_exp = jnp.where(frame_valid, jnp.exp(cross_scores - cross_max), 0.0)
+    cross_probs = cross_exp / jnp.sum(cross_exp, axis=-1, keepdims=True)
+    cross_probs_low = rounded(cross_probs)
+    attended_cross = jnp.einsum(
+        "qbhk,kbhd->qbhd", cross_probs_low, memory_value_heads, preferred_element_type=jnp.float32
+    )
+    attended_cross_low = rounded(attended_cross.reshape(token_count, D))
+    after_rows = (
+        middle_rows
+        + project(attended_cross_low, full_cross_out)
+        + full_cross_out_bias.astype(jnp.float32)
+    )
+    normed_mlp, scaled_mlp, inverse_mlp = norm_forward(
+        after_rows, full_mlp_gain.astype(jnp.float32), full_mlp_shift.astype(jnp.float32)
+    )
+    normed_mlp_low = rounded(normed_mlp)
+    hidden_pre = project(normed_mlp_low, full_fc_in) + full_fc_in_bias.astype(jnp.float32)
+    activated, gelu_pull = jax.vjp(exact_gelu, hidden_pre)
+    activated_low = rounded(activated)
+    result_rows = (
+        after_rows + project(activated_low, full_fc_out) + full_fc_out_bias.astype(jnp.float32)
+    )
+    output = rounded(result_rows).reshape(local_len, batch_count, D)
+    back_fc_in, back_fc_out = full_fc_in, full_fc_out
+    grad_result = out_grad.reshape(token_count, D)
+    grad_mlp_low = rounded(grad_result)
+    grad_fc_out_weight = weight_grad(activated_low, grad_mlp_low)
+    grad_fc_out_bias = column_sums(grad_mlp_low)
+    grad_activated = project_back(grad_mlp_low, back_fc_out)
+    grad_hidden_low = rounded(gelu_pull(grad_activated)[0])
+    grad_fc_in_weight = weight_grad(normed_mlp_low, grad_hidden_low)
+    grad_fc_in_bias = column_sums(grad_hidden_low)
+    grad_normed_mlp = project_back(grad_hidden_low, back_fc_in)
+    grad_rows_mlp, grad_mlp_gain, grad_mlp_shift = norm_backward(
+        grad_normed_mlp, scaled_mlp, inverse_mlp, full_mlp_gain.astype(jnp.float32)
+    )
+    early_grads = jnp.concatenate(
+        (
+            jnp.transpose(
+                grad_fc_in_weight.astype(jnp.bfloat16).reshape(
+                    owners, shard_rows, wide_parts, D
+                ),
+                (0, 2, 1, 3),
+            ).reshape(owners, wide_parts * shard_rows, D),
+            grad_fc_out_weight.astype(jnp.bfloat16).reshape(owners, -1, D),
+        ),
+        axis=1,
+    )
+    owned_early = lax.psum_scatter(
+        early_grads, ("dp", "seq"), scatter_dimension=0, tiled=False
+    )
+    grad_after = grad_result + grad_rows_mlp
+    back_cross_query, back_cross_key, back_cross_value, back_cross_out = (
+        full_cross_query,
+        full_cross_key,
+        full_cross_value,
+        full_cross_out,
+    )
+    grad_cross_low = rounded(grad_after)
+    grad_cross_out_weight = weight_grad(attended_cross_low, grad_cross_low)
+    grad_cross_out_bias = column_sums(grad_cross_low)
+    grad_attended_cross = rounded(project_back(grad_cross_low, back_cross_out)).reshape(
+        local_len, batch_count, HEADS, HEAD
+    )
+    grad_cross_probs = jnp.einsum(
+        "qbhd,kbhd->qbhk",
+        grad_attended_cross,
+        memory_value_heads,
+        preferred_element_type=jnp.float32,
+    )
+    cross_delta = jnp.sum(cross_probs * grad_cross_probs, axis=-1, keepdims=True)
+    grad_cross_scores = rounded(cross_probs * (grad_cross_probs - cross_delta) * 0.125)
+    grad_cross_queries = rounded(
+        jnp.einsum(
+            "qbhk,kbhd->qbhd",
+            grad_cross_scores,
+            memory_key_heads,
+            preferred_element_type=jnp.float32,
+        ).reshape(token_count, D)
+    )
+    grad_memory_keys = jnp.einsum(
+        "qbhk,qbhd->kbhd", grad_cross_scores, cross_queries, preferred_element_type=jnp.float32
+    ).reshape(frame_count, batch_count, D)
+    grad_memory_values = jnp.einsum(
+        "qbhk,qbhd->kbhd", cross_probs_low, grad_attended_cross, preferred_element_type=jnp.float32
+    ).reshape(frame_count, batch_count, D)
+    grad_memory_kv = jnp.concatenate(
+        (grad_memory_keys.astype(jnp.bfloat16), grad_memory_values.astype(jnp.bfloat16)), axis=2
+    ).reshape(seq_count, frame_part, batch_count, 2 * D)
+    grad_memory_kv, owned_early = lax.optimization_barrier((grad_memory_kv, owned_early))
+    part_kv = lax.psum_scatter(grad_memory_kv, "seq", scatter_dimension=0, tiled=False)
+    wide_rows = wide_parts * shard_rows
+    owned_fc_in = jnp.transpose(
+        owned_early[:wide_rows].astype(jnp.float32).reshape(wide_parts, shard_rows, D), (1, 0, 2)
+    ).reshape(shard_rows, wide_parts * D)
+    owned_fc_out = owned_early[wide_rows:].astype(jnp.float32)
+    part_flat_keys = part_kv[:, :, :D].reshape(frame_part * batch_count, D)
+    part_flat_values = part_kv[:, :, D:].reshape(frame_part * batch_count, D)
+    part_memory_grad = (
+        project_back(part_flat_keys, back_cross_key)
+        + project_back(part_flat_values, back_cross_value)
+    ).reshape(frame_part, batch_count, D)
+    grad_cross_key_weight = weight_grad(memory_part, part_flat_keys)
+    grad_cross_value_weight = weight_grad(memory_part, part_flat_values)
+    grad_cross_value_bias = column_sums(part_flat_values)
+    grad_cross_query_weight = weight_grad(normed_cross_low, grad_cross_queries)
+    grad_cross_query_bias = column_sums(grad_cross_queries)
+    grad_normed_cross = project_back(grad_cross_queries, back_cross_query)
+    grad_rows_cross, grad_cross_gain, grad_cross_shift = norm_backward(
+        grad_normed_cross, scaled_cross, inverse_cross, full_cross_gain.astype(jnp.float32)
+    )
+    grad_middle = grad_after + grad_rows_cross
+    back_query, back_key, back_value, back_self_out = (
+        full_query,
+        full_key,
+        full_value,
+        full_self_out,
+    )
+    grad_self_low = rounded(grad_middle)
+    grad_attn_out_weight = weight_grad(attended_self_low, grad_self_low)
+    grad_attn_out_bias = column_sums(grad_self_low)
+    grad_attended_self = rounded(project_back(grad_self_low, back_self_out))
+    head_grad = lax.all_to_all(to_pairs(grad_attended_self, seq_count), "seq", 0, 0).reshape(
+        full_length, PAIR
+    )
+    head_grads = self_backward(
+        head_queries, head_keys, head_values, labels, head_attended, head_log, head_grad
+    )
+    grad_triple = lax.all_to_all(
+        jnp.stack(
+            tuple(part.reshape(seq_count, local_len, PAIR) for part in head_grads), axis=1
+        ),
+        "seq",
+        0,
+        0,
+    )
+    grad_query_low, grad_key_low, grad_value_low = (
+        from_pairs(grad_triple[:, slot]) for slot in range(3)
+    )
+    grad_query_weight = weight_grad(normed_self_low, grad_query_low)
+    grad_query_bias = column_sums(grad_query_low)
+    grad_key_weight = weight_grad(normed_self_low, grad_key_low)
+    grad_value_weight = weight_grad(normed_self_low, grad_value_low)
+    grad_value_bias = column_sums(grad_value_low)
+    grad_normed_self = (
+        project_back(grad_query_low, back_query)
+        + project_back(grad_key_low, back_key)
+        + project_back(grad_value_low, back_value)
+    )
+    grad_rows_self, grad_self_gain, grad_self_shift = norm_backward(
+        grad_normed_self, scaled_self, inverse_self, full_self_gain.astype(jnp.float32)
+    )
+    token_grad = (grad_middle + grad_rows_self).reshape(local_len, batch_count, D)
+    def owner_rows(matrix):
+        return matrix.astype(jnp.bfloat16).reshape(owners, -1, D)
+
+    late_vectors = jnp.concatenate(
+        tuple(
+            vector.reshape(owners, -1)
+            for vector in (
+                grad_self_gain,
+                grad_self_shift,
+                grad_query_bias,
+                grad_value_bias,
+                grad_attn_out_bias,
+                grad_cross_gain,
+                grad_cross_shift,
+                grad_cross_query_bias,
+                grad_cross_value_bias,
+                grad_cross_out_bias,
+                grad_mlp_gain,
+                grad_mlp_shift,
+                grad_fc_out_bias,
+                grad_fc_in_bias,
+            )
+        ),
+        axis=1,
+    )
+    late_block = jnp.pad(
+        late_vectors.astype(jnp.bfloat16),
+        ((0, 0), (0, vector_rows * D - late_vectors.shape[1])),
+    ).reshape(owners, vector_rows, D)
+    late_grads = jnp.concatenate(
+        (
+            owner_rows(grad_query_weight),
+            owner_rows(grad_key_weight),
+            owner_rows(grad_value_weight),
+            owner_rows(grad_attn_out_weight),
+            owner_rows(grad_cross_query_weight),
+            owner_rows(grad_cross_key_weight),
+            owner_rows(grad_cross_value_weight),
+            owner_rows(grad_cross_out_weight),
+            late_block,
+        ),
+        axis=1,
+    )
+    owned_late = lax.psum_scatter(
+        late_grads, ("dp", "seq"), scatter_dimension=0, tiled=False
+    ).astype(jnp.float32)
+    memory_grad = lax.all_gather(
+        part_memory_grad.astype(jnp.bfloat16), "seq", axis=0, tiled=True
+    ).astype(jnp.float32)
+    owned_vectors = owned_late[8 * shard_rows :].reshape(-1)
+
+    def own_square(slot):
+        return owned_late[slot * shard_rows : (slot + 1) * shard_rows]
+
+    def own_vector(slot):
+        return owned_vectors[slot * shard_rows : (slot + 1) * shard_rows]
+
+    owned_fc_in_bias = owned_vectors[13 * shard_rows : 13 * shard_rows + fc_in_bias.shape[0]]
+    return (
+        output,
+        token_grad,
+        memory_grad,
+        own_vector(0),
+        own_vector(1),
+        own_square(0),
+        own_vector(2),
+        own_square(1),
+        own_square(2),
+        own_vector(3),
+        own_square(3),
+        own_vector(4),
+        own_vector(5),
+        own_vector(6),
+        own_square(4),
+        own_vector(7),
+        own_square(5),
+        own_square(6),
+        own_vector(8),
+        own_square(7),
+        own_vector(9),
+        own_vector(10),
+        own_vector(11),
+        owned_fc_in,
+        owned_fc_in_bias,
+        owned_fc_out,
+        own_vector(12),
+    )
 
 
 def local(
@@ -633,4 +1267,8 @@
         P(("dp", "seq"), None),
         P(("dp", "seq")),
     )
-    return jax.shard_map(local, mesh=mesh, in_specs=in_specs, out_specs=out_specs, check_vma=False)
+    by_heads = D // PAIR <= mesh.shape["seq"] <= 8
+    return jax.shard_map(
+        local_heads if by_heads else local,
+        mesh=mesh, in_specs=in_specs, out_specs=out_specs, check_vma=False,
+    )

time: 1120 us -> 808 us (0.72)
  waiting for transfers between devices: 583 us -> 304 us
  matrix products: 203 us -> 118 us
  Pallas kernels: 0 us -> 76.5 us
  blocking collectives: 0 us -> 32.3 us
  local copies, waits for them, and re-layouts: 217 us -> 185 us
  other arithmetic: 83.7 us -> 52.6 us
  starting transfers between devices: 0.42 us -> 13.7 us
    reduce_scatter x3, waiting for transfers between devices: 349 us -> 166 us  [the longest x1 103 us: local_heads(): lax.psum_scatter(late_grads, ('dp', 'seq'), scatter_dimension=0, tiled=Fa...]
    all_gather x3, waiting for transfers between devices: 234 us -> 58 us  [the longest x1 58 us: local_heads(): first = lax.all_gather(first_packed, ('dp', 'seq'), axis=0, tiled=False)]
    dot_general x34 -> x6, matrix products: 135 us -> 51.9 us  [the longest x1 17.2 us: local_heads(): jnp.einsum('qbhd,kbhd->qbhk', grad_attended_cross, memory_value_heads, pr...]
    all_to_all x0 -> x3, waiting for transfers between devices: none -> 79.7 us  [the longest x1 56.6 us: local_heads(): lax.all_to_all(jnp.stack(tuple((to_pairs(rows, seq_count) for rows in (qu...]
    pallas_call x0 -> x2, Pallas kernels: none -> 76.5 us  [the longest x1 38.5 us: self_forward(): pl.pallas_call(self_forward_body, grid=(length // QUERY_BLOCK,), in_specs...]
    all_to_all x0 -> x1, blocking collectives: none -> 32.3 us  [local_heads(): lax.all_to_all(to_pairs(grad_attended_self, seq_count), 'seq', 0, 0)]
    dynamic_slice x16 -> x0, local copies, waits for them, and re-layouts: 20 us -> none  [the longest x4 9.4 us: fold_block(): lax.dynamic_slice_in_dim(value_piece, block_start, block_rows, 0)]
    concatenate x7 -> x4, local copies, waits for them, and re-layouts: 31 us -> 11.5 us  [the longest x1 9.59 us: local_heads(): jnp.concatenate((self_gain, self_shift, query_bias, value_bias, attn_out_...]
  transfers between devices with their start and end apart: 6 -> 9, of which waited for: 6 -> 6; matrix products, arithmetic and copies ran while one was open for 14% -> 30% of each run, Pallas kernels for 0% -> 10%
where the time goes in v2:
time: 808 us; the launch traced here: 799 us
  waiting for transfers between devices  304 us (38%)
  local copies, waits for them, and re-layouts  185 us (23%)
  matrix products  118 us (15%)
  Pallas kernels  76.5 us (9%)
  other arithmetic  52.6 us (7%)
  blocking collectives  32.3 us (4%)
  between operations  16.7 us (2%)
  starting transfers between devices  13.7 us (2%)
    reduce_scatter x1, waiting for transfers between devices, local_heads(): lax.psum_scatter(late_grads, ('dp', 'seq'), scatter_dimension=0, tiled=Fa...  103 us
    all_gather x1, waiting for transfers between devices, local_heads(): first = lax.all_gather(first_packed, ('dp', 'seq'), axis=0, tiled=False)  58 us
    reduce_scatter x1, waiting for transfers between devices, local_heads(): lax.psum_scatter(early_grads, ('dp', 'seq'), scatter_dimension=0, tiled=F...  57.7 us
    unnamed x223, local copies, waits for them, and re-layouts  57 us
    all_to_all x1, waiting for transfers between devices, local_heads(): lax.all_to_all(jnp.stack(tuple((to_pairs(rows, seq_count) for rows in (qu...  56.6 us
    pallas_call x1, Pallas kernels, self_forward(): pl.pallas_call(self_forward_body, grid=(length // QUERY_BLOCK,), in_specs...  38.5 us
    pallas_call x1, Pallas kernels, self_backward(): pl.pallas_call(self_backward_body, grid=(length // QUERY_BLOCK,), in_spec...  38 us
    all_to_all x1, blocking collectives, local_heads(): lax.all_to_all(to_pairs(grad_attended_self, seq_count), 'seq', 0, 0)  32.3 us
  transfers between devices with their start and end apart: 9, of which 6 were waited for; matrix products, arithmetic and copies ran while one was open for 30% of the time, Pallas kernels for 10%

profile of v2, /device:TPU:0, one launch (start us, length us, event | category | flops | bytes accessed | tf_op | source)
XLA Modules:
  0.0 799.0 jit_solution(9706804730185335828)
XLA Ops:
  7.3 9.6 %concatenate.23 = bf16[408]{0:T(512)(128)(2,1)S(1)} concatenate(bf16[24]{0:T(256)(128)(2,1)} %param.33, bf16[24]{0:T(256)(128)(2,1)} %param.34, bf16[24]{0:T(256)(128)(2,1)} %param.36, bf16[24]{0:T(256)(128)(2,1)} %param.39, bf16[24]{0:T(256)(128)(2,1)} %param.41, bf16[24]{0:T(256)(128)(2,1)} %param.42, bf16[24]{0:T(256)(128)(2,1)} %param.43, bf16[24]{0:T(256)(128)(2,1)} %param.45, ...), dimensions={0} | concatenate | bytes 1632 | tf_op jit(solution)/shard_map/concatenate | solution.py:326
  24.2 58.0 %all-gather.7.cloned.1.call-done = bf16[2560,768]{1,0:T(8,128)(2,1)} async-done(((bf16[80,768]{1,0:T(8,128)(2,1)}), bf16[2560,768]{1,0:T(8,128)(2,1)}) %all-gather.7.cloned.1.call-update) | async-done | bytes 3932176 | tf_op jit(solution)/shard_map/all_gather | solution.py:350
  88.2 3.7 fusion.90
  93.7 1.8 fusion.34
  96.5 2.6 convolution_convert_fusion.15
  102.8 4.4 all-to-all-start
  108.8 56.6 %all-to-all-done = bf16[8,3,256,128]{2,3,1,0:T(8,128)(2,1)} async-done(((bf16[8,3,256,128]{2,3,1,0:T(8,128)(2,1)}), bf16[8,3,256,128]{2,3,1,0:T(8,128)(2,1)}, u32[]{:S(2)}, u32[]{:S(2)}) %all-to-all-start) | async-done | bytes 1572896 | tf_op jit(solution)/shard_map/all_to_all | solution.py:417
  165.3 2.8 fusion.92
  168.1 2.2 copy.163
  170.3 2.0 copy.162
  173.3 38.5 %self_forward.1 = (f32[2048,128]{1,0:T(8,128)}, f32[2048,128]{1,0:T(8,128)}) custom-call(bf16[2048,128]{1,0:T(8,128)(2,1)} %bitcast.364, bf16[2048,128]{1,0:T(8,128)(2,1)} %bitcast.362, bf16[2048,128]{1,0:T(8,128)(2,1)} %bitcast.360, s32[2048,1]{1,0:T(8,128)} %copy.164.column_ref, s32[1,2048]{1,0:T(1,128)} %bitcast.429), custom_call_target="tpu_custom_call" | custom-call | tf_op jit(solution)/shard_map/self_forward/pallas_call | solution.py:174
  211.9 2.1 convert_element_type.406
  214.0 2.0 copy.165
  216.1 4.2 all-to-all-start.1
  236.8 4.9 fusion.89
  241.8 7.0 fusion.88
  248.7 2.3 copy.169
  251.1 3.2 copy.200
  258.3 3.5 convolution_convert_fusion.2
  261.8 3.6 add_convert_fusion
  265.4 4.9 fusion.4
  270.3 4.7 fusion.8
  275.1 2.3 copy-done.1
  277.4 7.4 fusion.37
  285.7 9.8 %multiply_convert_fusion = (bf16[256,3072]{1,0:T(8,128)(2,1)}, f32[256,3072]{1,0:T(8,128)S(1)}, f32[256,3072]{1,0:T(8,128)S(1)}) fusion(f32[3072]{0:T(1024)S(1)} %copy-done.79, bf16[768,3072]{1,0:T(8,128)(2,1)S(1)} %bitcast.371, f32[256,768]{1,0:T(8,128)S(1)} %get-tuple-element.256, f32[768]{0:T(1024)S(1)} %copy-done.49, f32[768]{0:T(1024)S(1)} %copy-done.47, ...), kind=kOutput, calls=%fused_computation.32 | convolution fusion | flops 1260847104 | bytes 13389824 | tf_op jit(solution)/shard_map/dot_general | solution.py:25
  295.5 2.6 fusion.96
  299.3 3.7 convolution_convert_fusion.1
  303.0 9.8 %reshape.859 = bf16[32,24,4,768]{3,2,1,0:T(4,128)(2,1)} reshape(bf16[768,3072]{1,0:T(8,128)(2,1)} %convolution_convert_fusion.1) | data formatting | bytes 9437184 | tf_op jit(solution)/shard_map/reshape | solution.py:507
  312.8 3.4 copy.183
  317.7 4.0 pad_maximum_fusion
  321.7 5.4 multiply_reduce_fusion
  330.4 11.3 %fusion.25 = bf16[1536,1,12,64]{0,3,2,1:T(8,128)(2,1)} fusion(bf16[256,12,64]{0,2,1:T(8,128)(2,1)} %bitcast.423, f32[256,12]{0,1:T(8,128)} %copy-done.50, f32[256,12]{0,1:T(8,128)S(1)} %get-tuple-element.253, f32[12,1536,256]{2,1,0:T(8,128)} %copy-done.1, pred[1536]{0:T(1024)(128)(4,1)} %iota_compare_fusion), kind=kOutput, calls=%fused_computation.47 | convolution fusion | flops 628752384 | bytes 21652992 | tf_op jit(solution)/shard_map/qbhk,qbhd->kbhd/dot_general | solution.py:551
  341.7 6.0 convert_element_type.460
  347.7 17.2 %fusion = (f32[256,12]{0,1:T(8,128)S(1)}, f32[12,1536,256]{2,1,0:T(8,128)}) fusion(f32[256,12]{0,1:T(8,128)} %copy-done.50, f32[256,12]{0,1:T(8,128)S(1)} %get-tuple-element.253, f32[12,1536,256]{2,1,0:T(8,128)} %copy-done.1, pred[1536]{0:T(1024)(128)(4,1)} %iota_compare_fusion, bf16[1536,12,64]{0,2,1:T(8,128)(2,1)} %bitcast.433, ...), kind=kOutput, calls=%fused_computation.2 | convolution fusion | flops 632288256 | bytes 40539648 | tf_op jit(solution)/shard_map/qbhd,kbhd->qbhk/dot_general | solution.py:532
  365.0 14.5 %fusion.9 = bf16[256,12,1536]{0,2,1:T(8,128)(2,1)S(1)} fusion(f32[12,1536,256]{2,1,0:T(8,128)} %get-tuple-element.260, f32[256,12]{0,1:T(8,128)S(1)} %get-tuple-element.259, f32[256,12]{0,1:T(8,128)S(1)} %copy-done.51, f32[256,12]{0,1:T(8,128)S(1)} %get-tuple-element.253, f32[12,1536,256]{2,1,0:T(8,128)} %copy-done.1, pred[1536]{0:T(1024)(128)(4,1)S(1)} %copy-done.55), kind=kLoop, calls=%fused_computation.13 | loop fusion | flops 37748736 | bytes 47224320 | tf_op jit(solution)/shard_map/reshape.20
  379.5 3.6 copy-done.2
  383.1 4.4 fusion.24
  387.5 6.0 convert_element_type.456
  393.5 8.2 %pad_maximum_fusion.1 = bf16[8,192,1,1536]{1,0,3,2:T(8,128)(2,1)} fusion(bf16[8,192,1,768]{1,0,3,2:T(8,128)(2,1)} %convert_element_type.460, bf16[8,192,1,768]{1,0,3,2:T(8,128)(2,1)} %convert_element_type.456), kind=kLoop, calls=%fused_computation.20 | loop fusion | flops 2359296 | bytes 9437184 | tf_op jit(solution)/shard_map/concatenate | solution.py:554
  401.7 57.7 %reduce-scatter.4.cloned.1.call-done = bf16[1,192,768]{2,1,0:T(8,128)(2,1)} async-done(((bf16[32,192,768]{2,1,0:T(8,128)(2,1)}), bf16[1,192,768]{2,1,0:T(8,128)(2,1)}) %reduce-scatter.4.cloned.1.call-update) | async-done | bytes 294928 | tf_op jit(solution)/shard_map/reduce_scatter | solution.py:516
  459.4 8.9 %copy.184 = bf16[8,192,1,1536]{3,1,2,0:T(8,128)(2,1)} copy(bf16[8,192,1,1536]{1,0,3,2:T(8,128)(2,1)} %pad_maximum_fusion.1) | data formatting | bytes 9437184 | tf_op jit(solution)/shard_map/optimization_barrier | solution.py:557
  468.4 6.8 bitcast_reduce_fusion.2
  480.8 32.3 %all_to_all.20 = bf16[8,256,128]{1,2,0:T(8,128)(2,1)} all-to-all(bf16[8,256,128]{1,2,0:T(8,128)(2,1)S(1)} %pad.25), channel_id=1, replica_groups=mesh['dp'=4,'seq'=8] {'seq'}, dimensions={0} | all-to-all | bytes 1048576 | tf_op jit(solution)/shard_map/all_to_all | solution.py:590
  513.1 2.0 copy.173
  515.2 38.0 %self_backward.1 = (bf16[2048,128]{1,0:T(8,128)(2,1)}, bf16[2048,128]{1,0:T(8,128)(2,1)}, bf16[2048,128]{1,0:T(8,128)(2,1)}) custom-call(bf16[2048,128]{1,0:T(8,128)(2,1)} %bitcast.365, bf16[2048,128]{1,0:T(8,128)(2,1)} %bitcast.363, bf16[2048,128]{1,0:T(8,128)(2,1)} %bitcast.361, s32[2048,1]{1,0:T(8,128)} %copy.164.column_ref, s32[1,2048]{1,0:T(1,128)} %bitcast.430, ...), custom_call_target="tpu_custom_call" | custom-call | tf_op jit(solution)/shard_map/self_backward/pallas_call | solution.py:262
  553.2 2.0 copy.175
  555.2 2.0 copy.176
  557.2 2.1 copy.177
  559.3 2.7 pad_maximum_fusion.3
  562.0 4.4 all-to-all-start.3
  566.5 2.7 convolution_convert_fusion.4
  569.2 2.7 convolution_convert_fusion.7
  572.0 5.2 reduce-scatter.6.cloned.1.call-done
  577.2 1.9 fusion.66
  579.1 2.6 fusion.40
  594.0 23.1 %all-to-all-done.3 = bf16[8,3,256,128]{2,3,1,0:T(8,128)(2,1)} async-done(((bf16[8,3,256,128]{2,3,1,0:T(8,128)(2,1)}), bf16[8,3,256,128]{2,3,1,0:T(8,128)(2,1)}, u32[]{:S(2)}, u32[]{:S(2)}) %all-to-all-start.3) | async-done | bytes 1572896 | tf_op jit(solution)/shard_map/all_to_all | solution.py:596
  617.2 2.0 bitcast_reduce_fusion
  621.3 2.0 fusion.97
  623.3 1.8 convolution_add_fusion.2
  625.1 2.2 fusion.53
  647.2 5.1 fusion.41
  655.9 2.1 bitcast_convert_fusion
  658.0 26.7 %copy.187 = f32[1536,1,768]{2,1,0:T(1,128)} copy(f32[1536,1,768]{2,0,1:T(8,128)S(1)} %bitcast_convert_fusion) | data formatting | bytes 9437184
  684.8 103.1 %reduce-scatter.8.cloned.1.call-done = bf16[1,200,768]{2,1,0:T(8,128)(2,1)} async-done(((bf16[32,200,768]{2,1,0:T(8,128)(2,1)}), bf16[1,200,768]{2,1,0:T(8,128)(2,1)}) %reduce-scatter.8.cloned.1.call-update) | async-done | bytes 307216 | tf_op jit(solution)/shard_map/reduce_scatter | solution.py:664
  (337 shorter events, 95.9 us)
Async XLA Ops:
  7.2 251.1 %copy-start = (bf16[1536,1,768]{2,0,1:T(8,128)(2,1)S(1)}, bf16[1536,1,768]{2,0,1:T(8,128)(2,1)}, u32[]{:S(2)}) copy-start(bf16[1536,1,768]{2,0,1:T(8,128)(2,1)} %param.30) | copy-start | bytes 7077892
  7.2 75.0 %all-gather.7.cloned.1.call-start = ((), (), s32[]{:S(2)}) async-start(), calls=%async_computation.10 | async-start | bytes 4055040 | tf_op jit(solution)/shard_map/all_gather | solution.py:350
  18.4 218.4 %all-gather.9.cloned.1.call-start = ((), (), s32[]{:S(2)}) async-start(), calls=%async_computation.11 | async-start | bytes 15814656 | tf_op jit(solution)/shard_map/all_gather | solution.py:370
  24.2 58.0 %copy-start.42 = (bf16[312,768]{1,0:T(8,128)(2,1)}, bf16[312,768]{1,0:T(8,128)(2,1)S(1)}, u32[]{:S(2)}) copy-start(bf16[312,768]{1,0:T(8,128)(2,1)S(1)} %constant_dynamic-update-slice_fusion) | copy-start | bytes 1437700
  83.4 13.1 %copy-start.80 = (f32[256]{0:T(256)}, f32[256]{0:T(256)S(1)}, u32[]{:S(2)}) copy-start(f32[256]{0:T(256)S(1)} %broadcast_multiply_fusion.8) | copy-start | bytes 3076
  84.6 11.8 %copy-start.87 = (f32[256]{0:T(256)}, f32[256]{0:T(256)S(1)}, u32[]{:S(2)}) copy-start(f32[256]{0:T(256)S(1)} %add_rsqrt_fusion.2) | copy-start | bytes 3076
  87.3 9.2 %copy-start.71 = (f32[768]{0:T(1024)}, f32[768]{0:T(1024)S(1)}, u32[]{:S(2)}) copy-start(f32[768]{0:T(1024)S(1)} %reshape.892) | copy-start | bytes 9220
  87.4 9.1 %copy-start.91 = (f32[768]{0:T(1024)}, f32[768]{0:T(1024)S(1)}, u32[]{:S(2)}) copy-start(f32[768]{0:T(1024)S(1)} %reshape.893) | copy-start | bytes 9220
  88.2 4.8 copy-start.16
  101.5 5.7 copy-start.97
  102.8 62.6 %all-to-all-start = ((bf16[8,3,256,128]{2,3,1,0:T(8,128)(2,1)}), bf16[8,3,256,128]{2,3,1,0:T(8,128)(2,1)}, u32[]{:S(2)}, u32[]{:S(2)}) async-start(bf16[8,3,256,128]{2,3,1,0:T(8,128)(2,1)} %copy.160), calls=%async_computation | async-start | bytes 3145728 | tf_op jit(solution)/shard_map/all_to_all | solution.py:417
  107.4 65.0 %copy-start.48 = (s32[2048]{0:T(1024)}, s32[2048]{0:T(1024)S(1)}, u32[]{:S(2)}) copy-start(s32[2048]{0:T(1024)S(1)} %fusion.72) | copy-start | bytes 24580
  173.3 47.8 %copy-start.20 = (f32[256,1,768]{2,1,0:T(1,128)S(1)}, f32[256,1,768]{2,1,0:T(1,128)}, u32[]{:S(2)}) copy-start(f32[256,1,768]{2,1,0:T(1,128)} %param.57) | copy-start | bytes 2359300
  211.9 22.5 %copy-start.53 = (f32[32,24]{1,0:T(8,128)S(1)}, f32[32,24]{1,0:T(8,128)}, u32[]{:S(2)}) copy-start(f32[32,24]{1,0:T(8,128)} %get-tuple-element.231) | copy-start | bytes 9220
  216.1 19.0 %all-to-all-start.1 = ((bf16[8,256,128]{1,2,0:T(8,128)(2,1)}), bf16[8,256,128]{1,2,0:T(8,128)(2,1)}, u32[]{:S(2)}, u32[]{:S(2)}) async-start(bf16[8,256,128]{1,2,0:T(8,128)(2,1)} %copy.165), calls=%async_computation.1 | async-start | bytes 1048576 | tf_op jit(solution)/shard_map/all_to_all | solution.py:429
  220.2 239.2 %reduce-scatter.4.cloned.1.call-start = ((), (), s32[]{:S(2)}) async-start(), calls=%async_computation.7 | async-start | bytes 9732096 | tf_op jit(solution)/shard_map/reduce_scatter | solution.py:516
  241.7 12.6 %copy-start.12 = (bf16[32,24,768]{2,1,0:T(8,128)(2,1)}, bf16[32,24,768]{2,1,0:T(8,128)(2,1)S(1)}, u32[]{:S(2)}) copy-start(bf16[32,24,768]{2,1,0:T(8,128)(2,1)S(1)} %get-tuple-element.204) | copy-start | bytes 3538948
  258.3 7.2 copy-start.18
  270.3 7.0 copy-start.1
  275.1 10.6 %slice-start = ((s8[4718592]{0:T(1024)(128)(4,1)}), s8[4194304]{0:T(1024)(128)(4,1)S(1)}, s32[]{:S(2)}) async-start(s8[4718592]{0:T(1024)(128)(4,1)} %bitcast.369), calls=%async_computation.13 | async-start | bytes 8388608
  277.3 7.4 copy-start.14
  277.3 7.4 copy-start.77
  277.3 8.3 %slice-start.1 = ((s8[4718592]{0:T(1024)(128)(4,1)}), s8[524288]{0:T(1024)(128)(4,1)S(1)}, s32[]{:S(2)}) async-start(s8[4718592]{0:T(1024)(128)(4,1)} %bitcast.369), calls=%async_computation.14 | async-start | bytes 1048576
  284.7 10.8 %copy-start.32 = (bf16[12,64,256]{2,1,0:T(8,128)(2,1)}, bf16[12,64,256]{2,1,0:T(8,128)(2,1)S(1)}, u32[]{:S(2)}) copy-start(bf16[12,64,256]{2,1,0:T(8,128)(2,1)S(1)} %fusion.37) | copy-start | bytes 1179652
  284.8 10.7 %slice-start.2 = ((s8[4718592]{0:T(1024)(128)(4,1)}), s8[4194304]{0:T(1024)(128)(4,1)S(1)}, s32[]{:S(2)}) async-start(s8[4718592]{0:T(1024)(128)(4,1)} %bitcast.378), calls=%async_computation.15 | async-start | bytes 8388608
  285.4 12.8 %copy-start.4 = (f32[256,768]{1,0:T(8,128)}, f32[256,768]{1,0:T(8,128)S(1)}, u32[]{:S(2)}) copy-start(f32[256,768]{1,0:T(8,128)S(1)} %get-tuple-element.256) | copy-start | bytes 2359300
  285.7 9.8 %slice-start.3 = ((s8[4718592]{0:T(1024)(128)(4,1)}), s8[524288]{0:T(1024)(128)(4,1)S(1)}, s32[]{:S(2)}) async-start(s8[4718592]{0:T(1024)(128)(4,1)} %bitcast.378), calls=%async_computation.16 | async-start | bytes 1048576
  285.7 9.8 %copy-start.39 = (bf16[256,1,768]{2,1,0:T(2,128)(2,1)S(1)}, bf16[256,1,768]{2,1,0:T(2,128)(2,1)}, u32[]{:S(2)}) copy-start(bf16[256,1,768]{2,1,0:T(2,128)(2,1)} %convert_element_type.441) | copy-start | bytes 1179652
  321.6 255.5 %reduce-scatter.6.cloned.1.call-start = ((), (), s32[]{:S(2)}) async-start(), calls=%async_computation.8 | async-start | bytes 5308416 | tf_op jit(solution)/shard_map/reduce_scatter | solution.py:558
  321.7 5.4 copy-start.5
  321.7 5.4 copy-start.22
  341.7 6.0 copy-start.45
  347.7 17.2 %copy-start.51 = (f32[256,12]{0,1:T(8,128)S(1)}, f32[256,12]{0,1:T(8,128)}, u32[]{:S(2)}) copy-start(f32[256,12]{0,1:T(8,128)} %copy-done.50) | copy-start | bytes 36868
  347.7 17.2 %copy-start.55 = (pred[1536]{0:T(1024)(128)(4,1)S(1)}, pred[1536]{0:T(1024)(128)(4,1)}, u32[]{:S(2)}) copy-start(pred[1536]{0:T(1024)(128)(4,1)} %iota_compare_fusion) | copy-start | bytes 4612
  364.9 18.2 %copy-start.19 = (bf16[256,768]{0,1:T(8,128)(2,1)S(1)}, bf16[256,768]{0,1:T(8,128)(2,1)}, u32[]{:S(2)}) copy-start(bf16[256,768]{0,1:T(8,128)(2,1)} %copy-done.18) | copy-start | bytes 1179652
  468.3 6.9 copy-start.36
  468.3 6.9 copy-start.57
  468.3 6.9 copy-start.70
  468.4 6.9 copy-start.85
  559.3 7.2 copy-start.33
  562.0 7.2 copy-start.76
  562.0 55.2 %all-to-all-start.3 = ((bf16[8,3,256,128]{2,3,1,0:T(8,128)(2,1)}), bf16[8,3,256,128]{2,3,1,0:T(8,128)(2,1)}, u32[]{:S(2)}, u32[]{:S(2)}) async-start(bf16[8,3,256,128]{2,3,1,0:T(8,128)(2,1)} %pad_maximum_fusion.3), calls=%async_computation.3 | async-start | bytes 3145728 | tf_op jit(solution)/shard_map/all_to_all | solution.py:596
  566.5 89.4 %all-gather.11.cloned.1.call-start = ((), (), s32[]{:S(2)}) async-start(), calls=%async_computation.12 | async-start | bytes 2654208 | tf_op jit(solution)/shard_map/all_gather | solution.py:667
  569.2 12.8 %copy-start.29 = (bf16[6,256,128]{1,2,0:T(8,128)(2,1)S(1)}, bf16[6,256,128]{1,2,0:T(8,128)(2,1)}, u32[]{:S(2)}) copy-start(bf16[6,256,128]{1,2,0:T(8,128)(2,1)} %slice.298) | copy-start | bytes 1179652
  572.0 10.1 %copy-start.8 = (f32[256,768]{1,0:T(8,128)S(1)}, f32[256,768]{1,0:T(8,128)}, u32[]{:S(2)}) copy-start(f32[256,768]{1,0:T(8,128)} %copy-done.7) | copy-start | bytes 2359300
  577.2 6.4 copy-start.86
  581.8 206.1 %reduce-scatter.8.cloned.1.call-start = ((), (), s32[]{:S(2)}) async-start(), calls=%async_computation.9 | async-start | bytes 10137600 | tf_op jit(solution)/shard_map/reduce_scatter | solution.py:664
  621.3 6.1 copy-start.43
  621.3 3.8 copy-start.17
  621.3 3.8 copy-start.38
  621.3 3.8 copy-start.72
  621.3 3.8 copy-start.81
  621.3 3.8 copy-start.88
  636.5 3.7 copy-start.58
  636.5 3.7 copy-start.59
  636.5 3.7 copy-start.60
  636.5 3.7 copy-start.61
  647.2 5.1 copy-start.96
  647.2 5.1 copy-start.95
  647.2 5.1 copy-start.9
  647.2 5.2 copy-start.40
  647.2 5.2 copy-start.74
  647.2 5.2 copy-start.83
  647.2 5.2 copy-start.90
  (47 other events, 112.6 us)
Sparse Core Ops, SparseCore 0:
  18.5 63.6 all-gather.6
  85.1 130.2 all-gather.8
  321.8 137.5 reduce-scatter.3
  468.4 108.6 reduce-scatter.5
  581.9 63.3 all-gather.10
  651.1 136.7 reduce-scatter.7
